TPU v7x, 32 devices: a whole 2x2x4 slice. The times are simulated.
32 devices in a mesh: ctx: 8 (over z, x), tp: 4 (over y, core).
Axes of the slice: x: 2, y: 2, z: 4, core: 2. Of those that a mesh axis runs over, the one named last changes fastest.
Arguments:
- query_heads: bfloat16 [2048, 32, 128], P('ctx', 'tp'), may hold values from -6 to 6
- key_heads: bfloat16 [2048, 4, 128], P('ctx', 'tp'), may hold values from -6 to 6
- value_heads: bfloat16 [2048, 4, 128], P('ctx', 'tp'), may hold values from -6 to 6
- attn_out: bfloat16 [2048, 32, 128], P('ctx', 'tp'), may hold values from -6 to 6
- log_sum_exp: float32 [2048, 32], P('ctx', 'tp'), as said below
- positions: int32 [2048], P('ctx'), may hold values from 0 to 2047, as said below
- layer_grad: bfloat16 [2048, 8192], P('ctx', 'tp'), may hold values from -6 to 6
- w_out: bfloat16 [4096, 8192], P('tp'), may hold values from -0.0625 to 0.0625
Outputs:
- query_grad: bfloat16 [2048, 32, 128], P('ctx', 'tp')
- key_grad: bfloat16 [2048, 4, 128], P('ctx', 'tp')
- value_grad: bfloat16 [2048, 4, 128], P('ctx', 'tp')
Inputs may be any that keep to these rules, and one draw needn't show every extreme that they name: The sequence is cut into 16 blocks of 128 consecutive positions; the 256 rows of each index of ctx are two whole blocks, numbers b and 15 - b, in either order; every position appears once. log_sum_exp[t, h] is the logarithm of the sum of exp(scores[h, t, u]) over all u with positions[u] <= positions[t].
All inputs are finite; a program needn't handle non-finite values.
Results may differ from a plain program's by a relative error of at most 0.0059.
Values may be sent and summed in bfloat16 or wider, within the bound.
No kernel may reach another device: no remote copies, remote signals or barrier semaphores. Data moves between devices by JAX's collectives and lax.ppermute only.
A program may use at most 64 MiB of HBM per device.

v0:
```python
import math

import jax
import jax.numpy as jnp
from jax import lax
from jax.sharding import PartitionSpec as P


def from_behind(x, axis, by):
    size = lax.axis_size(axis)
    return lax.ppermute(x, axis, [(i, (i + by) % size) for i in range(size)])


def block_grads(
    queries, grad_out, lse_rows, delta_rows, query_places, key_part, value_part, key_places
):
    score_scale = 1.0 / math.sqrt(queries.shape[-1])
    scores = (
        jnp.einsum("igre,jge->grij", queries, key_part, preferred_element_type=jnp.float32)
        * score_scale
    )
    visible = query_places[:, None] >= key_places[None, :]
    attn_probs = jnp.where(visible, jnp.exp(scores - lse_rows), 0.0)
    probs_half = attn_probs.astype(jnp.bfloat16)
    prob_grad = jnp.einsum(
        "igre,jge->grij", grad_out, value_part, preferred_element_type=jnp.float32
    )
    score_grad = (attn_probs * (prob_grad - delta_rows)).astype(jnp.bfloat16)
    query_term = jnp.einsum(
        "grij,jge->igre", score_grad, key_part, preferred_element_type=jnp.float32
    )
    key_term = jnp.einsum("grij,igre->jge", score_grad, queries, preferred_element_type=jnp.float32)
    value_term = jnp.einsum(
        "grij,igre->jge", probs_half, grad_out, preferred_element_type=jnp.float32
    )
    return (query_term, key_term, value_term)


def local(query_heads, key_heads, value_heads, attn_out, log_sum_exp, positions, layer_grad, w_out):
    row_count = query_heads.shape[0]
    kv_local = key_heads.shape[1]
    head_dim = key_heads.shape[2]
    group_size = query_heads.shape[1] // kv_local
    flat_grad = lax.dot_general(
        lax.all_gather(layer_grad, "tp", axis=1, tiled=True),
        w_out,
        (((1,), (1,)), ((), ())),
        preferred_element_type=jnp.float32,
    )
    grad_out = flat_grad.astype(jnp.bfloat16).reshape(row_count, kv_local, group_size, head_dim)
    shaped = query_heads.reshape(row_count, kv_local, group_size, head_dim)
    saved_out = attn_out.reshape(row_count, kv_local, group_size, head_dim)
    delta = jnp.sum(grad_out.astype(jnp.float32) * saved_out.astype(jnp.float32), axis=3)
    delta_rows = jnp.transpose(delta, (1, 2, 0))[..., None]
    lse_rows = jnp.transpose(log_sum_exp.reshape(row_count, kv_local, group_size), (1, 2, 0))[
        ..., None
    ]
    all_places = lax.all_gather(positions, "ctx", axis=0, tiled=True)
    my_index = lax.axis_index("ctx")
    cycle_size = lax.axis_size("ctx")

    def places_of(owner, offset, length):
        return lax.dynamic_slice_in_dim(all_places, owner * row_count + offset, length)

    def contribute(key_part, value_part, key_places):
        return block_grads(
            shaped, grad_out, lse_rows, delta_rows, positions, key_part, value_part, key_places
        )

    def pass_grads(grad_pair):
        return from_behind((grad_pair[0], grad_pair[1]), "ctx", 1)

    first_terms = contribute(key_heads, value_heads, positions)

    def cycle_turn(turn_index, loop_state):
        query_sum, kv_pair, grad_pair = loop_state
        kv_pair = from_behind((kv_pair[0], kv_pair[1]), "ctx", 1)
        grad_pair = pass_grads(grad_pair)
        owner = (my_index - turn_index) % cycle_size
        query_term, key_term, value_term = contribute(
            kv_pair[0], kv_pair[1], places_of(owner, 0, row_count)
        )
        return (
            query_sum + query_term,
            kv_pair,
            (grad_pair[0] + key_term, grad_pair[1] + value_term),
        )

    start_state = (first_terms[0], (key_heads, value_heads), (first_terms[1], first_terms[2]))
    query_sum, kv_pair, grad_pair = lax.fori_loop(1, cycle_size, cycle_turn, start_state)
    key_sum, value_sum = pass_grads(grad_pair)
    score_scale = 1.0 / math.sqrt(head_dim)
    query_grad = (
        (query_sum * score_scale)
        .astype(jnp.bfloat16)
        .reshape(row_count, kv_local * group_size, head_dim)
    )
    key_grad = (key_sum * score_scale).astype(jnp.bfloat16)
    value_grad = value_sum.astype(jnp.bfloat16)
    return (query_grad, key_grad, value_grad)


def solution(mesh):
    in_specs = (
        P("ctx", "tp", None),
        P("ctx", "tp", None),
        P("ctx", "tp", None),
        P("ctx", "tp", None),
        P("ctx", "tp"),
        P("ctx"),
        P("ctx", "tp"),
        P("tp", None),
    )
    out_specs = (P("ctx", "tp", None), P("ctx", "tp", None), P("ctx", "tp", None))
    return jax.shard_map(local, mesh=mesh, in_specs=in_specs, out_specs=out_specs, check_vma=False)
```

profile of v0, /device:TPU:0, one launch (start us, length us, event | category | flops | bytes accessed | tf_op | source)
XLA Modules:
  0.0 175.2 jit_solution(11103152488033121546)
XLA Ops:
  7.2 0.9 copy.82
  8.1 0.8 copy.83
  9.0 1.1 copy.60
  10.3 0.6 fusion.20
  10.9 1.1 convert_bitcast_fusion
  12.0 2.6 %copy.41 = bf16[8,256,256]{2,0,1:T(8,128)(2,1)} copy(bf16[8,256,256]{1,2,0:T(8,128)(2,1)} %convert_bitcast_fusion) | data formatting | bytes 2097152 | tf_op jit(solution)/shard_map/reshape.23
  14.6 22.3 %all-gather = s32[8,1,256]{2,1,0:T(1,128)S(1)} all-gather(s32[1,1,256]{2,1,0:T(1,128)S(1)} %bitcast.212), channel_id=1, replica_groups=mesh['ctx'=8,'tp'=4] {'ctx'}, dimensions={0}, use_global_device_ids=true | all-gather | bytes 9216 | tf_op jit(solution)/shard_map/all_gather | solution.py:58
  36.9 9.9 %all-gather.3.cloned.1.call-done = bf16[256,8192]{1,0:T(8,128)(2,1)} async-done(((bf16[256,2048]{1,0:T(8,128)(2,1)}), bf16[256,8192]{1,0:T(8,128)(2,1)}) %all-gather.3.cloned.1.call-update) | async-done | bytes 4194320 | tf_op jit(solution)/shard_map/all_gather | solution.py:45
  46.8 12.4 %convolution_convert_fusion = bf16[256,1024]{1,0:T(8,128)(2,1)} fusion(bf16[256,8192]{1,0:T(8,128)(2,1)} %all-gather.3.cloned.1.call-done, bf16[1024,8192]{1,0:T(8,128)(2,1)} %param.17), kind=kOutput, calls=%fused_computation.31 | convolution fusion | flops 4295229440 | bytes 21495808 | tf_op jit(solution)/shard_map/dot_general | solution.py:44
  59.1 1.1 copy.44
  60.3 1.4 multiply_reduce_fusion
  61.7 1.5 fusion.21
  63.3 1.1 convolution_bitcast_fusion.5
  65.0 1.6 convolution_bitcast_fusion.4
  66.7 92.0 %while.23 = (s32[]{:T(128)}, f32[256,1,8,128]{3,0,2,1:T(8,128)S(1)}, bf16[256,1,128]{2,0,1:T(8,128)(2,1)S(1)}, bf16[256,1,128]{2,0,1:T(8,128)(2,1)S(1)}, f32[256...) while((s32[]{:T(128)}, ...), condition=%wide.region_2.3_spmd, body=%wide.region_1.2_spmd.sunk | while | flops 675151872 | bytes 16339448 | solution.py:90
  66.7 1.5 collective-permute-start.1
  68.2 1.5 collective-permute-start
  69.7 1.5 collective-permute-start.3
  71.2 1.5 collective-permute-start.2
  72.8 2.9 %collective-permute-done = bf16[256,1,128]{2,0,1:T(8,128)(2,1)S(1)} collective-permute-done((bf16[256,1,128]{2,0,1:T(8,128)(2,1)S(1)}, bf16[256,1,128]{2,0,1:T(8,128)(2,1)S(1)}, u32[]{:S(2)}, u32[]{:S(2)}) %collective-permute-start) | collective-permute-done | bytes 65568 | tf_op jit(solution)/shard_map/while/body/eval_jaxpr/ppermute | solution.py:11
  76.7 0.6 fusion.67
  77.4 1.3 collective-permute-done.3
  79.2 1.6 collective-permute-done.2
  80.8 1.1 fusion.68
  81.9 1.1 collective-permute-start
  83.6 2.4 %collective-permute-start.2 = (f32[256,1,128]{2,0,1:T(8,128)}, f32[256,1,128]{2,0,1:T(8,128)S(1)}, u32[]{:S(2)}, u32[]{:S(2)}) collective-permute-start(f32[256,1,128]{2,0,1:T(8,128)} %get-tuple-element.471), channel_id=1, source_target_pairs={{0,4},{4,8},{8,12},{12,16},{16,20},{20,24},{24,28},{28,0},{1,5},{5... | collective-permute-start | bytes 393224 | tf_op jit(solution)/shard_map/while/body/eval_jaxpr/ppermute | solution.py:11
  86.2 4.8 %collective-permute-done = bf16[256,1,128]{2,0,1:T(8,128)(2,1)S(1)} collective-permute-done((bf16[256,1,128]{2,0,1:T(8,128)(2,1)S(1)}, bf16[256,1,128]{2,0,1:T(8,128)(2,1)S(1)}, u32[]{:S(2)}, u32[]{:S(2)}) %collective-permute-start) | collective-permute-done | bytes 65568 | tf_op jit(solution)/shard_map/while/body/eval_jaxpr/ppermute | solution.py:11
  92.0 0.6 fusion.67
  92.7 0.9 collective-permute-done.3
  94.0 1.0 collective-permute-done.2
  94.9 1.1 fusion.68
  96.0 2.5 %collective-permute-start.2 = (f32[256,1,128]{2,0,1:T(8,128)}, f32[256,1,128]{2,0,1:T(8,128)S(1)}, u32[]{:S(2)}, u32[]{:S(2)}) collective-permute-start(f32[256,1,128]{2,0,1:T(8,128)} %get-tuple-element.471), channel_id=1, source_target_pairs={{0,4},{4,8},{8,12},{12,16},{16,20},{20,24},{24,28},{28,0},{1,5},{5... | collective-permute-start | bytes 393224 | tf_op jit(solution)/shard_map/while/body/eval_jaxpr/ppermute | solution.py:11
  98.7 6.3 %collective-permute-done = bf16[256,1,128]{2,0,1:T(8,128)(2,1)S(1)} collective-permute-done((bf16[256,1,128]{2,0,1:T(8,128)(2,1)S(1)}, bf16[256,1,128]{2,0,1:T(8,128)(2,1)S(1)}, u32[]{:S(2)}, u32[]{:S(2)}) %collective-permute-start) | collective-permute-done | bytes 65568 | tf_op jit(solution)/shard_map/while/body/eval_jaxpr/ppermute | solution.py:11
  106.1 0.6 fusion.67
  107.2 0.9 collective-permute-done.2
  108.2 1.1 fusion.68
  109.3 1.4 collective-permute-start.2
  110.9 6.9 %collective-permute-done = bf16[256,1,128]{2,0,1:T(8,128)(2,1)S(1)} collective-permute-done((bf16[256,1,128]{2,0,1:T(8,128)(2,1)S(1)}, bf16[256,1,128]{2,0,1:T(8,128)(2,1)S(1)}, u32[]{:S(2)}, u32[]{:S(2)}) %collective-permute-start) | collective-permute-done | bytes 65568 | tf_op jit(solution)/shard_map/while/body/eval_jaxpr/ppermute | solution.py:11
  118.8 0.6 fusion.67
  120.0 0.6 collective-permute-done.2
  120.6 1.1 fusion.68
  121.7 2.3 %collective-permute-start.2 = (f32[256,1,128]{2,0,1:T(8,128)}, f32[256,1,128]{2,0,1:T(8,128)S(1)}, u32[]{:S(2)}, u32[]{:S(2)}) collective-permute-start(f32[256,1,128]{2,0,1:T(8,128)} %get-tuple-element.471), channel_id=1, source_target_pairs={{0,4},{4,8},{8,12},{12,16},{16,20},{20,24},{24,28},{28,0},{1,5},{5... | collective-permute-start | bytes 393224 | tf_op jit(solution)/shard_map/while/body/eval_jaxpr/ppermute | solution.py:11
  124.2 5.2 %collective-permute-done = bf16[256,1,128]{2,0,1:T(8,128)(2,1)S(1)} collective-permute-done((bf16[256,1,128]{2,0,1:T(8,128)(2,1)S(1)}, bf16[256,1,128]{2,0,1:T(8,128)(2,1)S(1)}, u32[]{:S(2)}, u32[]{:S(2)}) %collective-permute-start) | collective-permute-done | bytes 65568 | tf_op jit(solution)/shard_map/while/body/eval_jaxpr/ppermute | solution.py:11
  130.4 0.6 fusion.67
  131.5 0.6 collective-permute-done.2
  132.2 1.1 fusion.68
  133.5 1.9 %collective-permute-start.3 = (f32[256,1,128]{2,0,1:T(8,128)S(1)}, f32[256,1,128]{2,0,1:T(8,128)S(1)}, u32[]{:S(2)}, u32[]{:S(2)}) collective-permute-start(f32[256,1,128]{2,0,1:T(8,128)S(1)} %get-tuple-element.472), channel_id=1, source_target_pairs={{0,4},{4,8},{8,12},{12,16},{16,20},{20,24},{24,28},{28,0},{1,5},{5... | collective-permute-start | bytes 393224 | tf_op jit(solution)/shard_map/while/body/eval_jaxpr/ppermute | solution.py:11
  135.4 1.6 collective-permute-start.2
  137.2 3.7 %collective-permute-done = bf16[256,1,128]{2,0,1:T(8,128)(2,1)S(1)} collective-permute-done((bf16[256,1,128]{2,0,1:T(8,128)(2,1)S(1)}, bf16[256,1,128]{2,0,1:T(8,128)(2,1)S(1)}, u32[]{:S(2)}, u32[]{:S(2)}) %collective-permute-start) | collective-permute-done | bytes 65568 | tf_op jit(solution)/shard_map/while/body/eval_jaxpr/ppermute | solution.py:11
  141.9 0.6 fusion.67
  143.1 0.6 collective-permute-done.2
  143.7 1.1 fusion.68
  144.8 2.6 %collective-permute-start = (bf16[256,1,128]{2,0,1:T(8,128)(2,1)S(1)}, bf16[256,1,128]{2,0,1:T(8,128)(2,1)S(1)}, u32[]{:S(2)}, u32[]{:S(2)}) collective-permute-start(bf16[256,1,128]{2,0,1:T(8,128)(2,1)S(1)} %get-tuple-element.469), channel_id=1, source_target_pairs={{0,4},{4,8},{8,12},{12,16},{16,20},{20,24},{24,28},{28,0},{1,5},{5... | collective-permute-start | bytes 196616 | tf_op jit(solution)/shard_map/while/body/eval_jaxpr/ppermute | solution.py:11
  147.8 1.4 collective-permute-start.2
  149.4 3.1 %collective-permute-done = bf16[256,1,128]{2,0,1:T(8,128)(2,1)S(1)} collective-permute-done((bf16[256,1,128]{2,0,1:T(8,128)(2,1)S(1)}, bf16[256,1,128]{2,0,1:T(8,128)(2,1)S(1)}, u32[]{:S(2)}, u32[]{:S(2)}) %collective-permute-start) | collective-permute-done | bytes 65568 | tf_op jit(solution)/shard_map/while/body/eval_jaxpr/ppermute | solution.py:11
  153.5 0.6 fusion.67
  154.2 0.9 collective-permute-done.3
  155.5 2.1 %collective-permute-done.2 = f32[256,1,128]{2,0,1:T(8,128)S(1)} collective-permute-done((f32[256,1,128]{2,0,1:T(8,128)}, f32[256,1,128]{2,0,1:T(8,128)S(1)}, u32[]{:S(2)}, u32[]{:S(2)}) %collective-permute-start.2) | collective-permute-done | bytes 131104 | tf_op jit(solution)/shard_map/while/body/eval_jaxpr/ppermute | solution.py:11
  157.6 1.1 fusion.68
  159.3 1.5 fusion.23
  160.8 4.9 %collective-permute-done.5 = bf16[256,1,128]{2,0,1:T(8,128)(2,1)S(1)} collective-permute-done((bf16[256,1,128]{2,0,1:T(8,128)(2,1)S(1)}, bf16[256,1,128]{2,0,1:T(8,128)(2,1)S(1)}, u32[]{:S(2)}, u32[]{:S(2)}) %collective-permute-start.5) | collective-permute-done | bytes 65568 | tf_op jit(solution)/shard_map/ppermute | solution.py:11
  165.7 1.4 collective-permute-done.4
  167.1 0.6 multiply_convert_fusion
  167.7 0.6 copy.84
  (94 shorter events, 14.4 us)
Async XLA Ops:
  7.2 3.1 %copy-start = (bf16[256,8,128]{2,1,0:T(8,128)(2,1)S(1)}, bf16[256,8,128]{2,1,0:T(8,128)(2,1)}, u32[]{:S(2)}) copy-start(bf16[256,8,128]{2,1,0:T(8,128)(2,1)} %param.10) | copy-start | bytes 1572868
  7.2 3.1 %copy-start.3 = (f32[256,8]{0,1:T(8,128)S(1)}, f32[256,8]{0,1:T(8,128)}, u32[]{:S(2)}) copy-start(f32[256,8]{0,1:T(8,128)} %param.14) | copy-start | bytes 24580
  7.2 2.9 %copy-start.2 = (s32[256]{0:T(256)S(1)}, s32[256]{0:T(256)}, u32[]{:S(2)}) copy-start(s32[256]{0:T(256)} %param.15) | copy-start | bytes 3076
  7.2 39.6 %all-gather.3.cloned.1.call-start = ((), (), s32[]{:S(2)}) async-start(), calls=%async_computation | async-start | bytes 5242880 | tf_op jit(solution)/shard_map/all_gather | solution.py:45
  61.7 1.6 copy-start.1
  66.7 9.6 %collective-permute-start.1 = (bf16[256,1,128]{2,0,1:T(8,128)(2,1)S(1)}, bf16[256,1,128]{2,0,1:T(8,128)(2,1)S(1)}, u32[]{:S(2)}, u32[]{:S(2)}) collective-permute-start(bf16[256,1,128]{2,0,1:T(8,128)(2,1)S(1)} %get-tuple-element.470), channel_id=1, source_target_pairs={{0,4},{4,8},{8,12},{12,16},{16,20},{20,24},{24,28},{28,0},{1,5},{5... | collective-permute-start | bytes 196616 | tf_op jit(solution)/shard_map/while/body/eval_jaxpr/ppermute | solution.py:11
  68.2 7.5 %collective-permute-start = (bf16[256,1,128]{2,0,1:T(8,128)(2,1)S(1)}, bf16[256,1,128]{2,0,1:T(8,128)(2,1)S(1)}, u32[]{:S(2)}, u32[]{:S(2)}) collective-permute-start(bf16[256,1,128]{2,0,1:T(8,128)(2,1)S(1)} %get-tuple-element.469), channel_id=1, source_target_pairs={{0,4},{4,8},{8,12},{12,16},{16,20},{20,24},{24,28},{28,0},{1,5},{5... | collective-permute-start | bytes 196616 | tf_op jit(solution)/shard_map/while/body/eval_jaxpr/ppermute | solution.py:11
  69.7 9.1 %collective-permute-start.3 = (f32[256,1,128]{2,0,1:T(8,128)S(1)}, f32[256,1,128]{2,0,1:T(8,128)S(1)}, u32[]{:S(2)}, u32[]{:S(2)}) collective-permute-start(f32[256,1,128]{2,0,1:T(8,128)S(1)} %get-tuple-element.472), channel_id=1, source_target_pairs={{0,4},{4,8},{8,12},{12,16},{16,20},{20,24},{24,28},{28,0},{1,5},{5... | collective-permute-start | bytes 393224 | tf_op jit(solution)/shard_map/while/body/eval_jaxpr/ppermute | solution.py:11
  71.2 9.6 %collective-permute-start.2 = (f32[256,1,128]{2,0,1:T(8,128)}, f32[256,1,128]{2,0,1:T(8,128)S(1)}, u32[]{:S(2)}, u32[]{:S(2)}) collective-permute-start(f32[256,1,128]{2,0,1:T(8,128)} %get-tuple-element.471), channel_id=1, source_target_pairs={{0,4},{4,8},{8,12},{12,16},{16,20},{20,24},{24,28},{28,0},{1,5},{5... | collective-permute-start | bytes 393224 | tf_op jit(solution)/shard_map/while/body/eval_jaxpr/ppermute | solution.py:11
  81.9 9.7 %collective-permute-start.1 = (bf16[256,1,128]{2,0,1:T(8,128)(2,1)S(1)}, bf16[256,1,128]{2,0,1:T(8,128)(2,1)S(1)}, u32[]{:S(2)}, u32[]{:S(2)}) collective-permute-start(bf16[256,1,128]{2,0,1:T(8,128)(2,1)S(1)} %get-tuple-element.470), channel_id=1, source_target_pairs={{0,4},{4,8},{8,12},{12,16},{16,20},{20,24},{24,28},{28,0},{1,5},{5... | collective-permute-start | bytes 196616 | tf_op jit(solution)/shard_map/while/body/eval_jaxpr/ppermute | solution.py:11
  81.9 9.1 %collective-permute-start = (bf16[256,1,128]{2,0,1:T(8,128)(2,1)S(1)}, bf16[256,1,128]{2,0,1:T(8,128)(2,1)S(1)}, u32[]{:S(2)}, u32[]{:S(2)}) collective-permute-start(bf16[256,1,128]{2,0,1:T(8,128)(2,1)S(1)} %get-tuple-element.469), channel_id=1, source_target_pairs={{0,4},{4,8},{8,12},{12,16},{16,20},{20,24},{24,28},{28,0},{1,5},{5... | collective-permute-start | bytes 196616 | tf_op jit(solution)/shard_map/while/body/eval_jaxpr/ppermute | solution.py:11
  83.0 10.5 %collective-permute-start.3 = (f32[256,1,128]{2,0,1:T(8,128)S(1)}, f32[256,1,128]{2,0,1:T(8,128)S(1)}, u32[]{:S(2)}, u32[]{:S(2)}) collective-permute-start(f32[256,1,128]{2,0,1:T(8,128)S(1)} %get-tuple-element.472), channel_id=1, source_target_pairs={{0,4},{4,8},{8,12},{12,16},{16,20},{20,24},{24,28},{28,0},{1,5},{5... | collective-permute-start | bytes 393224 | tf_op jit(solution)/shard_map/while/body/eval_jaxpr/ppermute | solution.py:11
  83.6 11.3 %collective-permute-start.2 = (f32[256,1,128]{2,0,1:T(8,128)}, f32[256,1,128]{2,0,1:T(8,128)S(1)}, u32[]{:S(2)}, u32[]{:S(2)}) collective-permute-start(f32[256,1,128]{2,0,1:T(8,128)} %get-tuple-element.471), channel_id=1, source_target_pairs={{0,4},{4,8},{8,12},{12,16},{16,20},{20,24},{24,28},{28,0},{1,5},{5... | collective-permute-start | bytes 393224 | tf_op jit(solution)/shard_map/while/body/eval_jaxpr/ppermute | solution.py:11
  96.0 9.7 %collective-permute-start.1 = (bf16[256,1,128]{2,0,1:T(8,128)(2,1)S(1)}, bf16[256,1,128]{2,0,1:T(8,128)(2,1)S(1)}, u32[]{:S(2)}, u32[]{:S(2)}) collective-permute-start(bf16[256,1,128]{2,0,1:T(8,128)(2,1)S(1)} %get-tuple-element.470), channel_id=1, source_target_pairs={{0,4},{4,8},{8,12},{12,16},{16,20},{20,24},{24,28},{28,0},{1,5},{5... | collective-permute-start | bytes 196616 | tf_op jit(solution)/shard_map/while/body/eval_jaxpr/ppermute | solution.py:11
  96.0 9.1 %collective-permute-start = (bf16[256,1,128]{2,0,1:T(8,128)(2,1)S(1)}, bf16[256,1,128]{2,0,1:T(8,128)(2,1)S(1)}, u32[]{:S(2)}, u32[]{:S(2)}) collective-permute-start(bf16[256,1,128]{2,0,1:T(8,128)(2,1)S(1)} %get-tuple-element.469), channel_id=1, source_target_pairs={{0,4},{4,8},{8,12},{12,16},{16,20},{20,24},{24,28},{28,0},{1,5},{5... | collective-permute-start | bytes 196616 | tf_op jit(solution)/shard_map/while/body/eval_jaxpr/ppermute | solution.py:11
  96.0 10.8 %collective-permute-start.3 = (f32[256,1,128]{2,0,1:T(8,128)S(1)}, f32[256,1,128]{2,0,1:T(8,128)S(1)}, u32[]{:S(2)}, u32[]{:S(2)}) collective-permute-start(f32[256,1,128]{2,0,1:T(8,128)S(1)} %get-tuple-element.472), channel_id=1, source_target_pairs={{0,4},{4,8},{8,12},{12,16},{16,20},{20,24},{24,28},{28,0},{1,5},{5... | collective-permute-start | bytes 393224 | tf_op jit(solution)/shard_map/while/body/eval_jaxpr/ppermute | solution.py:11
  96.0 12.2 %collective-permute-start.2 = (f32[256,1,128]{2,0,1:T(8,128)}, f32[256,1,128]{2,0,1:T(8,128)S(1)}, u32[]{:S(2)}, u32[]{:S(2)}) collective-permute-start(f32[256,1,128]{2,0,1:T(8,128)} %get-tuple-element.471), channel_id=1, source_target_pairs={{0,4},{4,8},{8,12},{12,16},{16,20},{20,24},{24,28},{28,0},{1,5},{5... | collective-permute-start | bytes 393224 | tf_op jit(solution)/shard_map/while/body/eval_jaxpr/ppermute | solution.py:11
  109.3 9.1 %collective-permute-start.1 = (bf16[256,1,128]{2,0,1:T(8,128)(2,1)S(1)}, bf16[256,1,128]{2,0,1:T(8,128)(2,1)S(1)}, u32[]{:S(2)}, u32[]{:S(2)}) collective-permute-start(bf16[256,1,128]{2,0,1:T(8,128)(2,1)S(1)} %get-tuple-element.470), channel_id=1, source_target_pairs={{0,4},{4,8},{8,12},{12,16},{16,20},{20,24},{24,28},{28,0},{1,5},{5... | collective-permute-start | bytes 196616 | tf_op jit(solution)/shard_map/while/body/eval_jaxpr/ppermute | solution.py:11
  109.3 8.5 %collective-permute-start = (bf16[256,1,128]{2,0,1:T(8,128)(2,1)S(1)}, bf16[256,1,128]{2,0,1:T(8,128)(2,1)S(1)}, u32[]{:S(2)}, u32[]{:S(2)}) collective-permute-start(bf16[256,1,128]{2,0,1:T(8,128)(2,1)S(1)} %get-tuple-element.469), channel_id=1, source_target_pairs={{0,4},{4,8},{8,12},{12,16},{16,20},{20,24},{24,28},{28,0},{1,5},{5... | collective-permute-start | bytes 196616 | tf_op jit(solution)/shard_map/while/body/eval_jaxpr/ppermute | solution.py:11
  109.3 10.3 %collective-permute-start.3 = (f32[256,1,128]{2,0,1:T(8,128)S(1)}, f32[256,1,128]{2,0,1:T(8,128)S(1)}, u32[]{:S(2)}, u32[]{:S(2)}) collective-permute-start(f32[256,1,128]{2,0,1:T(8,128)S(1)} %get-tuple-element.472), channel_id=1, source_target_pairs={{0,4},{4,8},{8,12},{12,16},{16,20},{20,24},{24,28},{28,0},{1,5},{5... | collective-permute-start | bytes 393224 | tf_op jit(solution)/shard_map/while/body/eval_jaxpr/ppermute | solution.py:11
  109.3 11.3 %collective-permute-start.2 = (f32[256,1,128]{2,0,1:T(8,128)}, f32[256,1,128]{2,0,1:T(8,128)S(1)}, u32[]{:S(2)}, u32[]{:S(2)}) collective-permute-start(f32[256,1,128]{2,0,1:T(8,128)} %get-tuple-element.471), channel_id=1, source_target_pairs={{0,4},{4,8},{8,12},{12,16},{16,20},{20,24},{24,28},{28,0},{1,5},{5... | collective-permute-start | bytes 393224 | tf_op jit(solution)/shard_map/while/body/eval_jaxpr/ppermute | solution.py:11
  121.7 8.3 %collective-permute-start.1 = (bf16[256,1,128]{2,0,1:T(8,128)(2,1)S(1)}, bf16[256,1,128]{2,0,1:T(8,128)(2,1)S(1)}, u32[]{:S(2)}, u32[]{:S(2)}) collective-permute-start(bf16[256,1,128]{2,0,1:T(8,128)(2,1)S(1)} %get-tuple-element.470), channel_id=1, source_target_pairs={{0,4},{4,8},{8,12},{12,16},{16,20},{20,24},{24,28},{28,0},{1,5},{5... | collective-permute-start | bytes 196616 | tf_op jit(solution)/shard_map/while/body/eval_jaxpr/ppermute | solution.py:11
  121.7 7.7 %collective-permute-start = (bf16[256,1,128]{2,0,1:T(8,128)(2,1)S(1)}, bf16[256,1,128]{2,0,1:T(8,128)(2,1)S(1)}, u32[]{:S(2)}, u32[]{:S(2)}) collective-permute-start(bf16[256,1,128]{2,0,1:T(8,128)(2,1)S(1)} %get-tuple-element.469), channel_id=1, source_target_pairs={{0,4},{4,8},{8,12},{12,16},{16,20},{20,24},{24,28},{28,0},{1,5},{5... | collective-permute-start | bytes 196616 | tf_op jit(solution)/shard_map/while/body/eval_jaxpr/ppermute | solution.py:11
  121.7 9.4 %collective-permute-start.3 = (f32[256,1,128]{2,0,1:T(8,128)S(1)}, f32[256,1,128]{2,0,1:T(8,128)S(1)}, u32[]{:S(2)}, u32[]{:S(2)}) collective-permute-start(f32[256,1,128]{2,0,1:T(8,128)S(1)} %get-tuple-element.472), channel_id=1, source_target_pairs={{0,4},{4,8},{8,12},{12,16},{16,20},{20,24},{24,28},{28,0},{1,5},{5... | collective-permute-start | bytes 393224 | tf_op jit(solution)/shard_map/while/body/eval_jaxpr/ppermute | solution.py:11
  121.7 10.5 %collective-permute-start.2 = (f32[256,1,128]{2,0,1:T(8,128)}, f32[256,1,128]{2,0,1:T(8,128)S(1)}, u32[]{:S(2)}, u32[]{:S(2)}) collective-permute-start(f32[256,1,128]{2,0,1:T(8,128)} %get-tuple-element.471), channel_id=1, source_target_pairs={{0,4},{4,8},{8,12},{12,16},{16,20},{20,24},{24,28},{28,0},{1,5},{5... | collective-permute-start | bytes 393224 | tf_op jit(solution)/shard_map/while/body/eval_jaxpr/ppermute | solution.py:11
  133.2 8.3 %collective-permute-start.1 = (bf16[256,1,128]{2,0,1:T(8,128)(2,1)S(1)}, bf16[256,1,128]{2,0,1:T(8,128)(2,1)S(1)}, u32[]{:S(2)}, u32[]{:S(2)}) collective-permute-start(bf16[256,1,128]{2,0,1:T(8,128)(2,1)S(1)} %get-tuple-element.470), channel_id=1, source_target_pairs={{0,4},{4,8},{8,12},{12,16},{16,20},{20,24},{24,28},{28,0},{1,5},{5... | collective-permute-start | bytes 196616 | tf_op jit(solution)/shard_map/while/body/eval_jaxpr/ppermute | solution.py:11
  133.2 7.7 %collective-permute-start = (bf16[256,1,128]{2,0,1:T(8,128)(2,1)S(1)}, bf16[256,1,128]{2,0,1:T(8,128)(2,1)S(1)}, u32[]{:S(2)}, u32[]{:S(2)}) collective-permute-start(bf16[256,1,128]{2,0,1:T(8,128)(2,1)S(1)} %get-tuple-element.469), channel_id=1, source_target_pairs={{0,4},{4,8},{8,12},{12,16},{16,20},{20,24},{24,28},{28,0},{1,5},{5... | collective-permute-start | bytes 196616 | tf_op jit(solution)/shard_map/while/body/eval_jaxpr/ppermute | solution.py:11
  133.5 9.2 %collective-permute-start.3 = (f32[256,1,128]{2,0,1:T(8,128)S(1)}, f32[256,1,128]{2,0,1:T(8,128)S(1)}, u32[]{:S(2)}, u32[]{:S(2)}) collective-permute-start(f32[256,1,128]{2,0,1:T(8,128)S(1)} %get-tuple-element.472), channel_id=1, source_target_pairs={{0,4},{4,8},{8,12},{12,16},{16,20},{20,24},{24,28},{28,0},{1,5},{5... | collective-permute-start | bytes 393224 | tf_op jit(solution)/shard_map/while/body/eval_jaxpr/ppermute | solution.py:11
  135.4 8.3 %collective-permute-start.2 = (f32[256,1,128]{2,0,1:T(8,128)}, f32[256,1,128]{2,0,1:T(8,128)S(1)}, u32[]{:S(2)}, u32[]{:S(2)}) collective-permute-start(f32[256,1,128]{2,0,1:T(8,128)} %get-tuple-element.471), channel_id=1, source_target_pairs={{0,4},{4,8},{8,12},{12,16},{16,20},{20,24},{24,28},{28,0},{1,5},{5... | collective-permute-start | bytes 393224 | tf_op jit(solution)/shard_map/while/body/eval_jaxpr/ppermute | solution.py:11
  144.8 8.3 %collective-permute-start.1 = (bf16[256,1,128]{2,0,1:T(8,128)(2,1)S(1)}, bf16[256,1,128]{2,0,1:T(8,128)(2,1)S(1)}, u32[]{:S(2)}, u32[]{:S(2)}) collective-permute-start(bf16[256,1,128]{2,0,1:T(8,128)(2,1)S(1)} %get-tuple-element.470), channel_id=1, source_target_pairs={{0,4},{4,8},{8,12},{12,16},{16,20},{20,24},{24,28},{28,0},{1,5},{5... | collective-permute-start | bytes 196616 | tf_op jit(solution)/shard_map/while/body/eval_jaxpr/ppermute | solution.py:11
  144.8 7.7 %collective-permute-start = (bf16[256,1,128]{2,0,1:T(8,128)(2,1)S(1)}, bf16[256,1,128]{2,0,1:T(8,128)(2,1)S(1)}, u32[]{:S(2)}, u32[]{:S(2)}) collective-permute-start(bf16[256,1,128]{2,0,1:T(8,128)(2,1)S(1)} %get-tuple-element.469), channel_id=1, source_target_pairs={{0,4},{4,8},{8,12},{12,16},{16,20},{20,24},{24,28},{28,0},{1,5},{5... | collective-permute-start | bytes 196616 | tf_op jit(solution)/shard_map/while/body/eval_jaxpr/ppermute | solution.py:11
  147.4 7.7 %collective-permute-start.3 = (f32[256,1,128]{2,0,1:T(8,128)S(1)}, f32[256,1,128]{2,0,1:T(8,128)S(1)}, u32[]{:S(2)}, u32[]{:S(2)}) collective-permute-start(f32[256,1,128]{2,0,1:T(8,128)S(1)} %get-tuple-element.472), channel_id=1, source_target_pairs={{0,4},{4,8},{8,12},{12,16},{16,20},{20,24},{24,28},{28,0},{1,5},{5... | collective-permute-start | bytes 393224 | tf_op jit(solution)/shard_map/while/body/eval_jaxpr/ppermute | solution.py:11
  147.8 9.8 %collective-permute-start.2 = (f32[256,1,128]{2,0,1:T(8,128)}, f32[256,1,128]{2,0,1:T(8,128)S(1)}, u32[]{:S(2)}, u32[]{:S(2)}) collective-permute-start(f32[256,1,128]{2,0,1:T(8,128)} %get-tuple-element.471), channel_id=1, source_target_pairs={{0,4},{4,8},{8,12},{12,16},{16,20},{20,24},{24,28},{28,0},{1,5},{5... | collective-permute-start | bytes 393224 | tf_op jit(solution)/shard_map/while/body/eval_jaxpr/ppermute | solution.py:11
  158.7 7.0 %collective-permute-start.5 = (bf16[256,1,128]{2,0,1:T(8,128)(2,1)S(1)}, bf16[256,1,128]{2,0,1:T(8,128)(2,1)S(1)}, u32[]{:S(2)}, u32[]{:S(2)}) collective-permute-start(bf16[256,1,128]{2,0,1:T(8,128)(2,1)S(1)} %convert.5), channel_id=1, source_target_pairs={{0,4},{4,8},{8,12},{12,16},{16,20},{20,24},{24,28},{28,0},{1,5},{5... | collective-permute-start | bytes 196616 | tf_op jit(solution)/shard_map/ppermute | solution.py:11
  158.8 8.4 %collective-permute-start.4 = (f32[256,1,128]{2,0,1:T(8,128)}, f32[256,1,128]{2,0,1:T(8,128)S(1)}, u32[]{:S(2)}, u32[]{:S(2)}) collective-permute-start(f32[256,1,128]{2,0,1:T(8,128)} %get-tuple-element.315), channel_id=1, source_target_pairs={{0,4},{4,8},{8,12},{12,16},{16,20},{20,24},{24,28},{28,0},{1,5},{5... | collective-permute-start | bytes 393224 | tf_op jit(solution)/shard_map/ppermute | solution.py:11
Sparse Core Ops, SparseCore 0:
  9.6 37.1 all-gather.2
where the time goes:
time: 176 us; the launch traced here: 175 us
  waiting for transfers between devices  59.7 us (34%)
  matrix products  39.9 us (23%)
  starting transfers between devices  25.1 us (14%)
  blocking collectives  22.3 us (13%)
  between operations  14.2 us (8%)
  local copies, waits for them, and re-layouts  8.15 us (5%)
  other arithmetic  5.47 us (3%)
    ppermute x30, waiting for transfers between devices, from_behind(): return lax.ppermute(x, axis, [(i, (i + by) % size) for i in range(size)])  49.8 us
    ppermute x30, starting transfers between devices, from_behind(): return lax.ppermute(x, axis, [(i, (i + by) % size) for i in range(size)])  25 us
    all_gather x1, blocking collectives, local(): all_places = lax.all_gather(positions, 'ctx', axis=0, tiled=True)  22.3 us
    dot_general x1, matrix products, local(): lax.dot_general(lax.all_gather(layer_grad, 'tp', axis=1, tiled=True), w_o...  12.4 us
    all_gather x1, waiting for transfers between devices, local(): lax.all_gather(layer_grad, 'tp', axis=1, tiled=True)  9.88 us
    dot_general x8, matrix products, block_grads(): jnp.einsum('grij,igre->jge', score_grad, queries, preferred_element_type=...  8.56 us
    dot_general x8, matrix products, block_grads(): jnp.einsum('grij,jge->igre', score_grad, key_part, preferred_element_type...  4.95 us
    dot_general x8, matrix products, block_grads(): jnp.einsum('igre,jge->grij', grad_out, value_part, preferred_element_type...  4.68 us
  transfers between devices with their start and end apart: 31, of which 20 were waited for; matrix products, arithmetic and copies ran while one was open for 13% of the time, Pallas kernels for 0%

commit v1 on v0

v1 whole, which is shorter than its diff:
```python
import functools
import math

import jax
import jax.numpy as jnp
from jax import lax
from jax.experimental import pallas as pl
from jax.experimental.pallas import tpu as pltpu
from jax.sharding import PartitionSpec as P


BF16 = jnp.bfloat16
F32 = jnp.float32
NT = (((1,), (1,)), ((), ()))
VMEM = pl.BlockSpec(memory_space=pltpu.VMEM)
HBM = pl.BlockSpec(memory_space=pltpu.HBM)
SMEM = pl.BlockSpec(memory_space=pltpu.SMEM)
MIB = 1 << 20


def swap(x, axis, bits):
    size = lax.axis_size(axis)
    return lax.ppermute(x, axis, [(i, i ^ bits) for i in range(size)])


def call(kernel, out_shape, in_specs, args, scratch=(), limit=16 * MIB, flops=0, size=0, exps=0):
    return pl.pallas_call(
        kernel,
        out_shape=out_shape,
        in_specs=in_specs,
        out_specs=jax.tree.map(lambda _: VMEM, out_shape),
        scratch_shapes=scratch,
        compiler_params=pltpu.CompilerParams(vmem_limit_bytes=limit),
        cost_estimate=pl.CostEstimate(flops=flops, bytes_accessed=size, transcendentals=exps),
    )(*args)


def shape(dims, dtype):
    return jax.ShapeDtypeStruct(dims, dtype)


def starts_of(pos_ref, half):
    high = jnp.where(pos_ref[0] > pos_ref[half], 0, half)
    return pl.multiple_of(high, half), pl.multiple_of(half - high, half)


def block_number(pos_ref, half):
    return lax.div(jnp.minimum(pos_ref[0], pos_ref[half]), jnp.int32(half))


def prep_kernel(half, pos_ref, lg_ref, k_ref, v_ref, high_ref, low_ref, own_ref, sem):
    high, low = starts_of(pos_ref, half)
    pieces = [
        (lg_ref.at[pl.ds(high, half)], high_ref),
        (lg_ref.at[pl.ds(low, half)], low_ref),
        (k_ref.at[pl.ds(low, half)], own_ref.at[pl.ds(0, half)]),
        (v_ref.at[pl.ds(low, half)], own_ref.at[pl.ds(half, half)]),
        (k_ref.at[pl.ds(high, half)], own_ref.at[pl.ds(2 * half, half)]),
        (v_ref.at[pl.ds(high, half)], own_ref.at[pl.ds(3 * half, half)]),
    ]
    copies = [pltpu.make_async_copy(a, b, sem.at[i]) for i, (a, b) in enumerate(pieces)]
    for copy in copies:
        copy.start()
    number = block_number(pos_ref, half).astype(F32)
    own_ref[pl.ds(4 * half, 16), :] = jnp.full((16, own_ref.shape[1]), number, F32).astype(BF16)
    for copy in copies:
        copy.wait()


def near_kernel(half, heads, hd, *refs):
    (pos_ref, tp_ref, w_ref, high_ref, low_ref, near_ref, q_ref, ao_ref, lse_ref) = refs[:9]
    outs = refs[9:19]
    w_buf, a_buf, raw, flat, acc, sem = refs[19:]
    acc_outs = outs[0:2]
    depth = high_ref.shape[1]
    parts = w_buf.shape[0]
    per = parts // 2
    width = depth // per
    high, low = starts_of(pos_ref, half)
    me = tp_ref[0]
    copies = []
    for i in range(parts):
        quarter = me if i < per else me ^ 1
        at = pl.multiple_of(quarter * depth + (i % per) * width, width)
        copies.append(pltpu.make_async_copy(w_ref.at[:, pl.ds(at, width)], w_buf.at[i], sem.at[i]))
    loads = [
        pltpu.make_async_copy(ref, raw.at[i], sem.at[parts + i])
        for i, ref in enumerate((q_ref, ao_ref))
    ]
    for copy in loads + copies:
        copy.start()

    a_buf[0, pl.ds(0, half), :] = high_ref[...]
    a_buf[0, pl.ds(half, half), :] = low_ref[...]
    a_buf[1, pl.ds(0, half), :] = near_ref[pl.ds(high, half), :]
    a_buf[1, pl.ds(half, half), :] = near_ref[pl.ds(low, half), :]

    for copy in loads:
        copy.wait()
    log2e = math.log2(math.e)
    for which, start in ((0, high), (1, low)):
        q_rows, q_t, ao_t, lse_row = outs[2 + 4 * which : 6 + 4 * which]
        first = pl.multiple_of(start * heads, half * heads)
        for source in (0, 1):
            flat[...] = raw[source, pl.ds(first, half * heads), :].astype(F32)
            for h in range(heads):
                at = pl.ds(h * half, half)
                rows = flat[pl.ds(h, half, stride=heads), :]
                if source == 0:
                    rows = rows.astype(BF16)
                    q_rows[at, :] = rows
                    q_t[:, at] = jnp.transpose(rows)
                else:
                    ao_t[:, at] = jnp.transpose(rows)
        for h in range(heads):
            lse_row[:, pl.ds(h * half, half)] = lse_ref[pl.ds(h, 1), pl.ds(start, half)] * log2e

    n = heads * hd
    for i in range(parts):
        copies[i].wait()
        a_part = a_buf[i // per, :, pl.ds((i % per) * width, width)]

        @pl.loop(0, n // 256)
        def _(block):
            at = pl.ds(pl.multiple_of(block * 256, 256), 256)
            term = lax.dot_general(w_buf[i, at, :], a_part, NT, preferred_element_type=F32)
            if i > 0:
                term = acc[at, :] + term
            if i < parts - 1:
                acc[at, :] = term
            else:
                acc_outs[0][at, :] = term[:, :half]
                acc_outs[1][at, :] = term[:, half:]


def far_kernel(load, *refs):
    if load:
        tp_ref, w_ref, acc_ref, part_ref, out_ref, w2_ref, w3_ref, sem = refs
        depth = part_ref.shape[1]
        copies = []
        for i, (ref, bits) in enumerate(((w2_ref, 2), (w3_ref, 3))):
            at = pl.multiple_of((tp_ref[0] ^ bits) * depth, depth)
            copies.append(pltpu.make_async_copy(w_ref.at[:, pl.ds(at, depth)], ref, sem.at[i]))
        for copy in copies:
            copy.start()
        copies[0].wait()
    else:
        acc_ref, part_ref, w2_ref, out_ref = refs

    @pl.loop(0, acc_ref.shape[0] // 256)
    def _(block):
        at = pl.ds(pl.multiple_of(block * 256, 256), 256)
        term = lax.dot_general(w2_ref[at, :], part_ref[...], NT, preferred_element_type=F32)
        out_ref[at, :] = acc_ref[at, :] + term

    if load:
        copies[1].wait()


def attend_kernel(high, slots, half, heads, hd, *refs):
    pos_ref, row_ref, acc_ref, part_ref, w_ref, q_rows, q_t, ao_t, lse_row = refs[:9]
    refs = refs[9:]
    kv_refs, refs = refs[:slots], refs[slots:]
    if high:
        dq_ref, far_ref, close_ref, even_ref, low_ref = refs[:5]
        refs = refs[5:]
    else:
        low_ref, dq_ref, far_ref, close_ref, even_ref = refs[:5]
        refs = refs[5:]
    k_buf, v_buf, do_rows, do_t, delta_row, dq_t, grads, p_buf, s_buf, listed = refs
    width = heads * half
    score_scale = 1.0 / math.sqrt(hd)
    factor = score_scale * math.log2(math.e)
    mine = block_number(pos_ref, half)

    count = jnp.int32(0)
    if high:
        for slot in range(slots):
            listed[slot] = jnp.int32(slot)
        count = jnp.int32(slots)
    for slot in range(1, slots):
        theirs = jnp.max(kv_refs[slot][pl.ds(4 * half, 16), :].astype(F32)).astype(jnp.int32)
        listed[count] = jnp.int32(slots + slot if high else slot)
        count = count + jnp.where((theirs > mine) if high else (theirs < mine), 1, 0)

    for slot in range(slots):
        at = pl.ds(slot * half, half)
        k_buf[at, :] = kv_refs[slot][pl.ds(0, half), :]
        v_buf[at, :] = kv_refs[slot][pl.ds(half, half), :]
        if high:
            at = pl.ds((slots + slot) * half, half)
            k_buf[at, :] = kv_refs[slot][pl.ds(2 * half, half), :]
            v_buf[at, :] = kv_refs[slot][pl.ds(3 * half, half), :]

    @pl.loop(0, heads)
    def _(h):
        at = pl.ds(pl.multiple_of(h * hd, hd), hd)
        to = pl.ds(pl.multiple_of(h * half, half), half)
        term = lax.dot_general(w_ref[at, :], part_ref[...], NT, preferred_element_type=F32)
        turned = (acc_ref[at, :] + term).astype(BF16)
        do_t[:, to] = turned
        do_rows[to, :] = jnp.transpose(turned)
        delta_row[:, to] = jnp.sum(turned.astype(F32) * ao_t[:, to], axis=0, keepdims=True)

    if high:
        grads[pl.ds(slots * half, slots * half), :] = jnp.zeros((slots * half, 2 * hd), F32)
    else:
        grads[...] = low_ref[...]

    def tile(keys, values, mask):
        m = keys.shape[0]
        keys_t = jnp.transpose(keys)
        for c in range(0, width, 2 * half):
            at = pl.ds(c, 2 * half)
            scores = jnp.dot(keys, q_t[:, at], preferred_element_type=F32)
            probs = jnp.exp2(scores * factor - lse_row[:, at])
            if mask is not None:
                probs = jnp.where(mask, probs, 0.0)
            prob_grad = jnp.dot(values, do_t[:, at], preferred_element_type=F32)
            p_buf[pl.ds(0, m), at] = probs.astype(BF16)
            s_buf[pl.ds(0, m), at] = (probs * (prob_grad - delta_row[:, at])).astype(BF16)
        value_term = jnp.dot(p_buf[pl.ds(0, m), :], do_rows[...], preferred_element_type=F32)
        key_term = jnp.dot(s_buf[pl.ds(0, m), :], q_rows[...], preferred_element_type=F32)
        for c in range(0, width, 2 * half):
            at = pl.ds(c, 2 * half)
            term = jnp.dot(keys_t, s_buf[pl.ds(0, m), at], preferred_element_type=F32)
            if mask is None:
                dq_t[:, at] += term
            else:
                dq_t[:, at] = term
        return key_term * score_scale, value_term

    def put(at, key_term, value_term):
        if not high:
            key_term = grads[at, pl.ds(0, hd)] + key_term
            value_term = grads[at, pl.ds(hd, hd)] + value_term
        grads[at, pl.ds(0, hd)] = key_term
        grads[at, pl.ds(hd, hd)] = value_term

    first, _ = starts_of(pos_ref, half)
    if not high:
        first = pl.multiple_of(half - first, half)
    places = jnp.broadcast_to(row_ref[:, pl.ds(first, half)].astype(F32), (half, half))
    visible = jnp.concatenate([places >= jnp.transpose(places)] * 2, axis=1)
    own = pl.ds(slots * half if high else 0, half)
    put(own, *tile(k_buf[own, :], v_buf[own, :], visible))

    def entry(i):
        return pl.ds(pl.multiple_of(listed[i] * half, half), half)

    @pl.loop(0, lax.div(count, jnp.int32(2)))
    def _(pair):
        one, two = entry(2 * pair), entry(2 * pair + 1)
        keys = jnp.concatenate([k_buf[one, :], k_buf[two, :]], axis=0)
        values = jnp.concatenate([v_buf[one, :], v_buf[two, :]], axis=0)
        key_term, value_term = tile(keys, values, None)
        put(one, key_term[:half], value_term[:half])
        put(two, key_term[half:], value_term[half:])

    @pl.when(lax.rem(count, jnp.int32(2)) == 1)
    def _():
        one = entry(count - 1)
        put(one, *tile(k_buf[one, :], v_buf[one, :], None))

    base = slots if high else 0
    for slot in range(slots):
        part = grads[pl.ds((base + slot) * half, half), :]
        place = (slot // 2) % (slots // 4)
        if slot % 2 == 0:
            even_ref[pl.ds(slot // 2 * half, half), :] = part
        else:
            ref = far_ref if slot >= slots // 2 else close_ref
            ref[pl.ds(place * half, half), :] = part.astype(BF16)
    if high:
        low_ref[...] = grads[pl.ds(0, slots * half), :]
    for h in range(heads):
        turned = jnp.transpose(dq_t[:, pl.ds(h * half, half)] * score_scale)
        dq_ref[h] = turned.astype(BF16)


def attend(high, positions, pos_row, acc, part, w3, sides, kv_parts, low_sums):
    slots = len(kv_parts)
    hd, width = sides[1].shape
    half = part.shape[0]
    heads = width // half
    entries = 2 * slots if high else slots
    args = [positions, pos_row, acc, part, w3, *sides, *kv_parts]
    out_shape = [
        shape((heads, half, hd), BF16),
        shape((slots // 4 * half, 2 * hd), BF16),
        shape((slots // 4 * half, 2 * hd), BF16),
        shape((slots // 2 * half, 2 * hd), F32),
    ]
    if high:
        out_shape.append(shape((slots * half, 2 * hd), F32))
    else:
        args.append(low_sums)
    blocks = slots * 3 // 2 if high else slots // 2
    return call(
        functools.partial(attend_kernel, high, slots, half, heads, hd),
        out_shape,
        [SMEM] + [VMEM] * (len(args) - 1),
        args,
        scratch=[
            pltpu.VMEM((entries * half, hd), BF16),
            pltpu.VMEM((entries * half, hd), BF16),
            pltpu.VMEM((width, hd), BF16),
            pltpu.VMEM((hd, width), BF16),
            pltpu.VMEM((1, width), F32),
            pltpu.VMEM((hd, width), F32),
            pltpu.VMEM((entries * half, 2 * hd), F32),
            pltpu.VMEM((2 * half, width), BF16),
            pltpu.VMEM((2 * half, width), BF16),
            pltpu.SMEM((2 * slots,), jnp.int32),
        ],
        limit=8 * MIB + entries * half * 2 * hd * 8,
        flops=20 * blocks * width * half * hd,
        size=4 * MIB,
        exps=blocks * width * half,
    )


def merge_kernel(half, even_ref, got_ref, *outs):
    for i, out in enumerate(outs):
        at = pl.ds(i * half, half)
        out[...] = (even_ref[at, :] + got_ref[at, :].astype(F32)).astype(out.dtype)


def merge(even, got, half, keep):
    n = got.shape[0] // half
    out_shape = [shape((half, got.shape[1]), F32 if keep and i == 0 else BF16) for i in range(n)]
    return call(
        functools.partial(merge_kernel, half),
        out_shape,
        [VMEM] * 2,
        [even, got],
        limit=4 * MIB,
        size=got.size * 8,
    )


def finish_kernel(count, half, hd, pos_ref, *refs):
    low, high = refs[:count], refs[count : 2 * count]
    dk_ref, dv_ref = refs[2 * count :]
    high_at, low_at = starts_of(pos_ref, half)
    for at, parts in ((low_at, low), (high_at, high)):
        total = parts[0][...]
        for part in parts[1:]:
            total = total + part[...].astype(F32)
        dk_ref[pl.ds(at, half), :] = total[:, :hd].astype(BF16)
        dv_ref[pl.ds(at, half), :] = total[:, hd:].astype(BF16)


def local(query_heads, key_heads, value_heads, attn_out, log_sum_exp, positions, layer_grad, w_out):
    rows, heads, hd = query_heads.shape
    half = rows // 2
    slots = lax.axis_size("ctx")
    depth = layer_grad.shape[1]
    n = w_out.shape[0]
    tp_index = lax.axis_index("tp").astype(jnp.int32).reshape(1)
    pos_row = positions.reshape(1, rows)

    near = swap(layer_grad, "tp", 1)
    lg_high, lg_low, own = call(
        functools.partial(prep_kernel, half),
        [
            shape((half, depth), BF16),
            shape((half, depth), BF16),
            shape((4 * half + 16, hd), BF16),
        ],
        [SMEM, HBM, HBM, HBM],
        [positions, layer_grad, key_heads.reshape(rows, hd), value_heads.reshape(rows, hd)],
        scratch=[pltpu.SemaphoreType.DMA((6,))],
        limit=62 * MIB,
        size=MIB,
    )
    far_high = swap(lg_high, "tp", 2)
    far_low = swap(lg_low, "tp", 2)

    kv_parts = [own] + [None] * (slots - 1)
    for slot in range(slots - 2, 0, -2):
        kv_parts[slot] = swap(own, "ctx", slot)
    for slot in range(0, slots, 2):
        kv_parts[slot + 1] = swap(kv_parts[slot], "ctx", 1)

    width = heads * half
    side = [
        shape((width, hd), BF16),
        shape((hd, width), BF16),
        shape((hd, width), F32),
        shape((1, width), F32),
    ]
    acc_high, acc_low, *sides = call(
        functools.partial(near_kernel, half, heads, hd),
        [shape((n, half), F32)] * 2 + side * 2,
        [SMEM, SMEM, HBM, VMEM, VMEM, VMEM, HBM, HBM, VMEM],
        [
            positions,
            tp_index,
            w_out,
            lg_high,
            lg_low,
            near,
            query_heads.reshape(rows * heads, hd),
            attn_out.reshape(rows * heads, hd),
            jnp.transpose(log_sum_exp),
        ],
        scratch=[
            pltpu.VMEM((4, n, depth // 2), BF16),
            pltpu.VMEM((2, rows, depth), BF16),
            pltpu.VMEM((2, rows * heads, hd), BF16),
            pltpu.VMEM((half * heads, hd), F32),
            pltpu.VMEM((n, rows), F32),
            pltpu.SemaphoreType.DMA((6,)),
        ],
        limit=46 * MIB,
        flops=4 * n * rows * depth,
        size=4 * n * depth,
    )
    relay_high = swap(far_high, "tp", 1)
    acc_high, w2, w3 = call(
        functools.partial(far_kernel, True),
        [shape((n, half), F32), shape((n, depth), BF16), shape((n, depth), BF16)],
        [SMEM, HBM, VMEM, VMEM],
        [tp_index, w_out, acc_high, far_high],
        scratch=[pltpu.SemaphoreType.DMA((2,))],
        limit=44 * MIB,
        flops=2 * n * half * depth,
        size=4 * n * depth,
    )
    dq_high, far_part, close_part, even_high, low_sums = attend(
        True, positions, pos_row, acc_high, relay_high, w3, sides[:4], kv_parts, None
    )
    x_far_high = swap(far_part, "ctx", 1)
    x_close_high = swap(close_part, "ctx", 1)

    relay_low = swap(far_low, "tp", 1)
    acc_low = call(
        functools.partial(far_kernel, False),
        shape((n, half), F32),
        [VMEM] * 3,
        [acc_low, far_low, w2],
        limit=4 * MIB,
        flops=2 * n * half * depth,
        size=2 * n * depth,
    )
    dq_low, far_part, close_part, even_low = attend(
        False, positions, pos_row, acc_low, relay_low, w3, sides[4:], kv_parts, low_sums
    )
    x_far_low = swap(far_part, "ctx", 1)
    x_close_low = swap(close_part, "ctx", 1)

    def z_stage(even, x_far, x_close):
        mid = slots // 4 * half
        far_sums = merge(even[mid:], x_far, half, False)
        close_sums = merge(even[:mid], x_close, half, True)
        got = [swap(x, "ctx", slots // 2 + 2 * i) for i, x in enumerate(far_sums)]
        got += [swap(x, "ctx", 2 * i + 2) for i, x in enumerate(close_sums[1:])]
        return [close_sums[0], *got]

    high_parts = z_stage(even_high, x_far_high, x_close_high)
    low_parts = z_stage(even_low, x_far_low, x_close_low)

    out = shape((rows, hd), BF16)
    key_grad, value_grad = call(
        functools.partial(finish_kernel, slots // 2, half, hd),
        [out, out],
        [SMEM] + [VMEM] * slots,
        [positions, *low_parts, *high_parts],
        limit=4 * MIB,
        size=2 * MIB,
    )
    first_high = positions[0] > positions[half]
    query_grad = jnp.concatenate(
        [
            jnp.where(first_high, dq_high, dq_low),
            jnp.where(first_high, dq_low, dq_high),
        ],
        axis=1,
    )
    query_grad = jnp.transpose(query_grad, (1, 0, 2))
    return (query_grad, key_grad[:, None, :], value_grad[:, None, :])


def solution(mesh):
    in_specs = (
        P("ctx", "tp", None),
        P("ctx", "tp", None),
        P("ctx", "tp", None),
        P("ctx", "tp", None),
        P("ctx", "tp"),
        P("ctx"),
        P("ctx", "tp"),
        P("tp", None),
    )
    out_specs = (P("ctx", "tp", None), P("ctx", "tp", None), P("ctx", "tp", None))

    return jax.shard_map(local, mesh=mesh, in_specs=in_specs, out_specs=out_specs, check_vma=False)
```

time: 176 us -> 91.9 us (0.52)
  waiting for transfers between devices: 59.7 us -> 18.8 us
  matrix products: 39.9 us -> 0 us
  Pallas kernels: 0 us -> 33.1 us
  blocking collectives: 22.3 us -> 0 us
  between operations: 14.2 us -> 2.09 us
  other arithmetic: 5.47 us -> 0.07 us
  starting transfers between devices: 25.1 us -> 29.4 us
    dot_general x41 -> x0, matrix products: 39.9 us -> none  [the longest x1 12.4 us: local(): lax.dot_general(lax.all_gather(layer_grad, 'tp', axis=1, tiled=True), w_o...]
    pallas_call x0 -> x11, Pallas kernels: none -> 33.1 us  [call(): pl.pallas_call(kernel, out_shape=out_shape, in_specs=in_specs, out_specs=...]
    ppermute x30 -> x22, waiting for transfers between devices: 49.8 us -> 18.8 us  [swap(): return lax.ppermute(x, axis, [(i, i ^ bits) for i in range(size)])]
    all_gather x1 -> x0, blocking collectives: 22.3 us -> none  [local(): all_places = lax.all_gather(positions, 'ctx', axis=0, tiled=True)]
    all_gather x1 -> x0, waiting for transfers between devices: 9.88 us -> none  [local(): lax.all_gather(layer_grad, 'tp', axis=1, tiled=True)]
    ppermute x30 -> x22, starting transfers between devices: 25 us -> 29.4 us  [swap(): return lax.ppermute(x, axis, [(i, i ^ bits) for i in range(size)])]
    another operation x1 -> x0, local copies, waits for them, and re-layouts: 2.64 us -> none
    unnamed x13 -> x17, local copies, waits for them, and re-layouts: 4.62 us -> 6.68 us
  transfers between devices with their start and end apart: 31 -> 22, of which waited for: 20 -> 8; matrix products, arithmetic and copies ran while one was open for 13% -> 3% of each run, Pallas kernels for 0% -> 30%
where the time goes in v1:
time: 91.9 us; the launch traced here: 91.4 us
  Pallas kernels  33.1 us (36%)
  starting transfers between devices  29.4 us (32%)
  waiting for transfers between devices  18.8 us (20%)
  local copies, waits for them, and re-layouts  8.03 us (9%)
  between operations  2.09 us (2%)
    pallas_call x11, Pallas kernels, call(): pl.pallas_call(kernel, out_shape=out_shape, in_specs=in_specs, out_specs=...  33.1 us
    ppermute x22, starting transfers between devices, swap(): return lax.ppermute(x, axis, [(i, i ^ bits) for i in range(size)])  29.4 us
    ppermute x22, waiting for transfers between devices, swap(): return lax.ppermute(x, axis, [(i, i ^ bits) for i in range(size)])  18.8 us
    unnamed x17, local copies, waits for them, and re-layouts  6.68 us
  transfers between devices with their start and end apart: 22, of which 8 were waited for; matrix products, arithmetic and copies ran while one was open for 3% of the time, Pallas kernels for 30%

profile of v1, /device:TPU:0, one launch (start us, length us, event | category | flops | bytes accessed | tf_op | source)
XLA Modules:
  0.0 91.4 jit_solution(5879233672306027190)
XLA Ops:
  0.6 0.6 collective-permute-start
  1.2 3.0 %shard_map.103 = (bf16[128,2048]{1,0:T(8,128)(2,1)}, bf16[128,2048]{1,0:T(8,128)(2,1)}, bf16[528,128]{1,0:T(8,128)(2,1)}) custom-call(s32[256]{0:T(256)} %pos_ref.3, bf16[256,2048]{1,0:T(8,128)(2,1)} %lg_ref.1, bf16[256,128]{1,0:T(8,128)(2,1)} %bitcast.17, bf16[256,128]{1,0:T(8,128)(2,1)} %bitcast.18), custom_call_target="tpu_custom_call" | custom-call | bytes 1048576 | tf_op jit(solution)/shard_map/pallas_call | solution.py:27
  4.2 2.6 %collective-permute-start.1 = (bf16[128,2048]{1,0:T(8,128)(2,1)}, bf16[128,2048]{1,0:T(8,128)(2,1)S(1)}, u32[]{:S(2)}, u32[]{:S(2)}) collective-permute-start(bf16[128,2048]{1,0:T(8,128)(2,1)} %get-tuple-element.38.refs_3_), channel_id=1, source_target_pairs={{0,2},{1,3},{2,0},{3,1},{4,6},{5,7},{6,4},{7,5},{8,10},{9,11},{10,... | collective-permute-start | bytes 1572872 | tf_op jit(solution)/shard_map/ppermute | solution.py:23
  6.7 0.1 collective-permute-start.10
  6.8 4.0 %collective-permute-start.8 = (bf16[528,128]{1,0:T(8,128)(2,1)}, bf16[528,128]{1,0:T(8,128)(2,1)S(1)}, u32[]{:S(2)}, u32[]{:S(2)}) collective-permute-start(bf16[528,128]{1,0:T(8,128)(2,1)} %get-tuple-element.47.refs_9_), channel_id=1, source_target_pairs={{0,24},{4,28},{8,16},{12,20},{16,8},{20,12},{24,0},{28,4},{1,25},{... | collective-permute-start | bytes 405512 | tf_op jit(solution)/shard_map/ppermute | solution.py:23
  10.8 0.0 collective-permute-start.6
  10.8 8.9 %collective-permute-done.1.refs_3_ = bf16[128,2048]{1,0:T(8,128)(2,1)S(1)} collective-permute-done((bf16[128,2048]{1,0:T(8,128)(2,1)}, bf16[128,2048]{1,0:T(8,128)(2,1)S(1)}, u32[]{:S(2)}, u32[]{:S(2)}) %collective-permute-start.1) | collective-permute-done | bytes 524320 | tf_op jit(solution)/shard_map/ppermute | solution.py:23
  19.7 0.0 collective-permute-start.2
  19.7 0.0 collective-permute-done.8.refs_15_
  19.7 2.1 %collective-permute-start.4 = (bf16[528,128]{1,0:T(8,128)(2,1)}, bf16[528,128]{1,0:T(8,128)(2,1)S(1)}, u32[]{:S(2)}, u32[]{:S(2)}) collective-permute-start(bf16[528,128]{1,0:T(8,128)(2,1)} %get-tuple-element.47.refs_9_), channel_id=1, source_target_pairs={{0,8},{4,12},{8,0},{12,4},{16,24},{20,28},{24,16},{28,20},{1,9},{5... | collective-permute-start | bytes 405512 | tf_op jit(solution)/shard_map/ppermute | solution.py:23
  21.8 0.8 collective-permute-done.6.refs_13_
  22.6 1.5 %collective-permute-start.3 = (bf16[528,128]{1,0:T(8,128)(2,1)}, bf16[528,128]{1,0:T(8,128)(2,1)S(1)}, u32[]{:S(2)}, u32[]{:S(2)}) collective-permute-start(bf16[528,128]{1,0:T(8,128)(2,1)} %get-tuple-element.47.refs_9_), channel_id=1, source_target_pairs={{0,4},{4,0},{8,12},{12,8},{16,20},{20,16},{24,28},{28,24},{1,5},{5... | collective-permute-start | bytes 405512 | tf_op jit(solution)/shard_map/ppermute | solution.py:23
  24.1 1.3 %fusion.2 = (s32[1]{0:T(128)}, s32[1]{0:T(128)}) fusion(s32[256]{0:T(256)} %pos_ref.3), kind=kLoop, calls=%fused_computation.5 | loop fusion | bytes 16 | tf_op jit(solution)/shard_map/slice | solution.py:473
  26.6 0.0 collective-permute-done.4.refs_11_
  26.6 1.3 %collective-permute-start.9 = (bf16[528,128]{1,0:T(8,128)(2,1)S(1)}, bf16[528,128]{1,0:T(8,128)(2,1)S(1)}, u32[]{:S(2)}, u32[]{:S(2)}) collective-permute-start(bf16[528,128]{1,0:T(8,128)(2,1)S(1)} %collective-permute-done.8.refs_15_), channel_id=1, source_target_pairs={{0,4},{4,0},{8,12},{12,8},{16,20},{20,16},{24,28},{28,24},{1,5},{5... | collective-permute-start | bytes 405512 | tf_op jit(solution)/shard_map/ppermute | solution.py:23
  27.9 0.0 collective-permute-done.3.refs_10_
  27.9 1.4 %collective-permute-start.7 = (bf16[528,128]{1,0:T(8,128)(2,1)S(1)}, bf16[528,128]{1,0:T(8,128)(2,1)S(1)}, u32[]{:S(2)}, u32[]{:S(2)}) collective-permute-start(bf16[528,128]{1,0:T(8,128)(2,1)S(1)} %collective-permute-done.6.refs_13_), channel_id=1, source_target_pairs={{0,4},{4,0},{8,12},{12,8},{16,20},{20,16},{24,28},{28,24},{1,5},{5... | collective-permute-start | bytes 405512 | tf_op jit(solution)/shard_map/ppermute | solution.py:23
  29.3 1.5 %collective-permute-done.10.refs_1_ = bf16[128,2048]{1,0:T(8,128)(2,1)S(1)} collective-permute-done((bf16[128,2048]{1,0:T(8,128)(2,1)}, bf16[128,2048]{1,0:T(8,128)(2,1)S(1)}, u32[]{:S(2)}, u32[]{:S(2)}) %collective-permute-start.10) | collective-permute-done | bytes 524320 | tf_op jit(solution)/shard_map/ppermute | solution.py:23
  30.8 1.7 %collective-permute-start.5 = (bf16[528,128]{1,0:T(8,128)(2,1)S(1)}, bf16[528,128]{1,0:T(8,128)(2,1)S(1)}, u32[]{:S(2)}, u32[]{:S(2)}) collective-permute-start(bf16[528,128]{1,0:T(8,128)(2,1)S(1)} %collective-permute-done.4.refs_11_), channel_id=1, source_target_pairs={{0,4},{4,0},{8,12},{12,8},{16,20},{20,16},{24,28},{28,24},{1,5},{5... | collective-permute-start | bytes 405512 | tf_op jit(solution)/shard_map/ppermute | solution.py:23
  32.5 0.0 collective-permute-done.refs_5_
  32.5 0.0 collective-permute-start.11
  32.5 0.0 copy-start
  32.5 1.0 %copy-done = bf16[256,8,128]{2,1,0:T(8,128)(2,1)S(1)} copy-done((bf16[256,8,128]{2,1,0:T(8,128)(2,1)S(1)}, bf16[256,8,128]{2,1,0:T(8,128)(2,1)}, u32[]{:S(2)}) %copy-start) | copy-done | bytes 524312
  33.5 1.0 %copy-done.1 = bf16[256,8,128]{2,1,0:T(8,128)(2,1)S(1)} copy-done((bf16[256,8,128]{2,1,0:T(8,128)(2,1)S(1)}, bf16[256,8,128]{2,1,0:T(8,128)(2,1)}, u32[]{:S(2)}) %copy-start.1) | copy-done | bytes 524312
  34.6 1.0 %copy-done.2 = bf16[128,2048]{1,0:T(8,128)(2,1)S(1)} copy-done((bf16[128,2048]{1,0:T(8,128)(2,1)S(1)}, bf16[128,2048]{1,0:T(8,128)(2,1)}, u32[]{:S(2)}) %copy-start.2) | copy-done | bytes 524312
  35.6 1.0 %copy-done.3 = bf16[128,2048]{1,0:T(8,128)(2,1)S(1)} copy-done((bf16[128,2048]{1,0:T(8,128)(2,1)S(1)}, bf16[128,2048]{1,0:T(8,128)(2,1)}, u32[]{:S(2)}) %copy-start.3) | copy-done | bytes 524312
  36.7 0.7 copy-done.5
  37.3 0.7 copy-done.7
  38.0 7.9 %shard_map.104 = (f32[1024,128]{1,0:T(8,128)S(1)}, f32[1024,128]{1,0:T(8,128)S(1)}, bf16[1024,128]{1,0:T(8,128)(2,1)S(1)}, bf16[128,1024]{1,0:T(8,128)(2,1)S(1)}...) custom-call(s32[256]{0:T(256)S(1)} %copy-done.5, ...), custom_call_target="tpu_custom_call" | custom-call | flops 2147483648 | bytes 8388608 | tf_op jit(solution)/shard_map/pallas_call | solution.py:27
  45.9 4.0 %shard_map.105 = (f32[1024,128]{1,0:T(8,128)S(1)}, bf16[1024,2048]{1,0:T(8,128)(2,1)S(1)}, bf16[1024,2048]{1,0:T(8,128)(2,1)S(1)}) custom-call(s32[1]{0:T(128)} %bitcast.2.refs_1_.refs_0_, bf16[1024,8192]{1,0:T(8,128)(2,1)} %refs_1_.1, f32[1024,128]{1,0:T(8,128)S(1)} %get-tuple-element.40.refs_2_, bf16[128,2048]{1,0:T(8,128)(2,1)S(1)} %collective-permute-done.1.refs_3_), custom_call_target="tpu_custom_call" | custom-call | flops 536870912 | bytes 8388608 | tf_op jit(solution)/shard_map/pallas_call | solution.py:27
  49.9 0.0 copy-start.4
  49.9 0.0 copy-start.6
  49.9 1.8 %shard_map.107.refs_2_ = f32[1024,128]{1,0:T(8,128)S(1)} custom-call(f32[1024,128]{1,0:T(8,128)S(1)} %get-tuple-element.49.refs_0_, bf16[128,2048]{1,0:T(8,128)(2,1)S(1)} %collective-permute-done.10.refs_1_, bf16[1024,2048]{1,0:T(8,128)(2,1)S(1)} %get-tuple-element.50.refs_2_), custom_call_target="tpu_custom_call" | custom-call | flops 536870912 | bytes 4194304 | tf_op jit(solution)/shard_map/pallas_call | solution.py:27
  51.7 0.0 collective-permute-done.9.refs_16_
  51.7 0.0 collective-permute-done.7.refs_14_
  51.7 0.0 collective-permute-done.5.refs_12_
  51.7 0.0 collective-permute-done.2.refs_3_
  51.7 0.0 copy-done.4
  51.8 0.0 copy-done.6
  51.8 10.8 %shard_map.106 = (bf16[8,128,128]{2,1,0:T(8,128)(2,1)S(1)}, bf16[256,256]{1,0:T(8,128)(2,1)S(1)}, bf16[256,256]{1,0:T(8,128)(2,1)S(1)}, f32[512,256]{1,0:T(8,128)S(1)}, f32[1024,256]{1,0:T(8,128)S(1)}) custom-call(s32[256]{0:T(256)S(1)} %copy-done.6, s32[1,256]{1,0:T(1,128)S(1)} %bitcast.14, f32[1024,128]{1,0:T(8,128)S(1)} %get-tuple-element.41.refs_2_, ...), custom_call_target="tpu_custom_call" | custom-call | flops 4026531840 | bytes 4194304 | tf_op jit(solution)/shard_map/pallas_call | solution.py:27
  62.6 0.0 collective-permute-done.11.refs_3_
  62.6 4.3 %shard_map.108 = (bf16[8,128,128]{2,1,0:T(8,128)(2,1)S(1)}, bf16[256,256]{1,0:T(8,128)(2,1)S(1)}, bf16[256,256]{1,0:T(8,128)(2,1)S(1)}, f32[512,256]{1,0:T(8,128)S(1)}) custom-call(s32[256]{0:T(256)S(1)} %copy-done.6, s32[1,256]{1,0:T(1,128)S(1)} %bitcast.15, f32[1024,128]{1,0:T(8,128)S(1)} %shard_map.107.refs_2_, ...), custom_call_target="tpu_custom_call" | custom-call | flops 1342177280 | bytes 4194304 | tf_op jit(solution)/shard_map/pallas_call | solution.py:27
  66.9 0.4 collective-permute-start.12
  67.3 1.7 %collective-permute-start.13 = (bf16[256,256]{1,0:T(8,128)(2,1)S(1)}, bf16[256,256]{1,0:T(8,128)(2,1)S(1)}, u32[]{:S(2)}, u32[]{:S(2)}) collective-permute-start(bf16[256,256]{1,0:T(8,128)(2,1)S(1)} %get-tuple-element.60), channel_id=1, source_target_pairs={{0,4},{4,0},{8,12},{12,8},{16,20},{20,16},{24,28},{28,24},{1,5},{5... | collective-permute-start | bytes 393224 | tf_op jit(solution)/shard_map/ppermute | solution.py:23
  69.0 0.3 collective-permute-start.17
  69.3 1.7 %collective-permute-start.18 = (bf16[256,256]{1,0:T(8,128)(2,1)S(1)}, bf16[256,256]{1,0:T(8,128)(2,1)S(1)}, u32[]{:S(2)}, u32[]{:S(2)}) collective-permute-start(bf16[256,256]{1,0:T(8,128)(2,1)S(1)} %get-tuple-element.67), channel_id=1, source_target_pairs={{0,4},{4,0},{8,12},{12,8},{16,20},{20,16},{24,28},{28,24},{1,5},{5... | collective-permute-start | bytes 393224 | tf_op jit(solution)/shard_map/ppermute | solution.py:23
  71.1 2.2 %collective-permute-done.12.got_ref = bf16[256,256]{1,0:T(8,128)(2,1)S(1)} collective-permute-done((bf16[256,256]{1,0:T(8,128)(2,1)S(1)}, bf16[256,256]{1,0:T(8,128)(2,1)S(1)}, u32[]{:S(2)}, u32[]{:S(2)}) %collective-permute-start.12) | collective-permute-done | bytes 131104 | tf_op jit(solution)/shard_map/ppermute | solution.py:23
  73.4 1.6 %collective-permute-start.16 = (bf16[128,256]{1,0:T(8,128)(2,1)S(1)}, bf16[128,256]{1,0:T(8,128)(2,1)S(1)}, u32[]{:S(2)}, u32[]{:S(2)}) collective-permute-start(bf16[128,256]{1,0:T(8,128)(2,1)S(1)} %get-tuple-element.63), channel_id=1, source_target_pairs={{0,8},{4,12},{8,0},{12,4},{16,24},{20,28},{24,16},{28,20},{1,9},{5... | collective-permute-start | bytes 196616 | tf_op jit(solution)/shard_map/ppermute | solution.py:23
  75.1 1.1 %collective-permute-done.13.got_ref = bf16[256,256]{1,0:T(8,128)(2,1)S(1)} collective-permute-done((bf16[256,256]{1,0:T(8,128)(2,1)S(1)}, bf16[256,256]{1,0:T(8,128)(2,1)S(1)}, u32[]{:S(2)}, u32[]{:S(2)}) %collective-permute-start.13) | collective-permute-done | bytes 131104 | tf_op jit(solution)/shard_map/ppermute | solution.py:23
  76.2 2.6 %collective-permute-start.14 = (bf16[128,256]{1,0:T(8,128)(2,1)S(1)}, bf16[128,256]{1,0:T(8,128)(2,1)S(1)}, u32[]{:S(2)}, u32[]{:S(2)}) collective-permute-start(bf16[128,256]{1,0:T(8,128)(2,1)S(1)} %get-tuple-element.61), channel_id=1, source_target_pairs={{0,16},{4,20},{8,24},{12,28},{16,0},{20,4},{24,8},{28,12},{1,17},{... | collective-permute-start | bytes 196616 | tf_op jit(solution)/shard_map/ppermute | solution.py:23
  78.8 1.4 %collective-permute-start.15 = (bf16[128,256]{1,0:T(8,128)(2,1)S(1)}, bf16[128,256]{1,0:T(8,128)(2,1)S(1)}, u32[]{:S(2)}, u32[]{:S(2)}) collective-permute-start(bf16[128,256]{1,0:T(8,128)(2,1)S(1)} %get-tuple-element.62), channel_id=1, source_target_pairs={{0,24},{4,28},{8,16},{12,20},{16,8},{20,12},{24,0},{28,4},{1,25},{... | collective-permute-start | bytes 196616 | tf_op jit(solution)/shard_map/ppermute | solution.py:23
  80.2 0.0 collective-permute-done.17.got_ref
  80.2 0.4 collective-permute-start.21
  80.6 0.6 collective-permute-done.18.got_ref
  81.3 2.7 %collective-permute-start.19 = (bf16[128,256]{1,0:T(8,128)(2,1)S(1)}, bf16[128,256]{1,0:T(8,128)(2,1)S(1)}, u32[]{:S(2)}, u32[]{:S(2)}) collective-permute-start(bf16[128,256]{1,0:T(8,128)(2,1)S(1)} %get-tuple-element.68), channel_id=1, source_target_pairs={{0,16},{4,20},{8,24},{12,28},{16,0},{20,4},{24,8},{28,12},{1,17},{... | collective-permute-start | bytes 196616 | tf_op jit(solution)/shard_map/ppermute | solution.py:23
  84.0 0.0 collective-permute-done.16.refs_3_
  84.0 1.4 %collective-permute-start.20 = (bf16[128,256]{1,0:T(8,128)(2,1)S(1)}, bf16[128,256]{1,0:T(8,128)(2,1)S(1)}, u32[]{:S(2)}, u32[]{:S(2)}) collective-permute-start(bf16[128,256]{1,0:T(8,128)(2,1)S(1)} %get-tuple-element.69), channel_id=1, source_target_pairs={{0,24},{4,28},{8,16},{12,20},{16,8},{20,12},{24,0},{28,4},{1,25},{... | collective-permute-start | bytes 196616 | tf_op jit(solution)/shard_map/ppermute | solution.py:23
  85.4 1.1 %copy.11 = bf16[256,8,128]{2,1,0:T(8,128)(2,1)} copy(bf16[256,8,128]{2,0,1:T(8,128)(2,1)S(1)} %maximum_bitcast_fusion) | data formatting | bytes 1048576
  86.5 0.0 collective-permute-done.14.refs_1_
  86.5 0.0 collective-permute-done.15.refs_2_
  86.5 0.0 collective-permute-done.21.refs_7_
  86.5 2.0 %collective-permute-done.19.refs_5_ = bf16[128,256]{1,0:T(8,128)(2,1)S(1)} collective-permute-done((bf16[128,256]{1,0:T(8,128)(2,1)S(1)}, bf16[128,256]{1,0:T(8,128)(2,1)S(1)}, u32[]{:S(2)}, u32[]{:S(2)}) %collective-permute-start.19) | collective-permute-done | bytes 65568 | tf_op jit(solution)/shard_map/ppermute | solution.py:23
  88.6 1.6 %collective-permute-done.20.refs_6_ = bf16[128,256]{1,0:T(8,128)(2,1)S(1)} collective-permute-done((bf16[128,256]{1,0:T(8,128)(2,1)S(1)}, bf16[128,256]{1,0:T(8,128)(2,1)S(1)}, u32[]{:S(2)}, u32[]{:S(2)}) %collective-permute-start.20) | collective-permute-done | bytes 65568 | tf_op jit(solution)/shard_map/ppermute | solution.py:23
  90.2 1.3 %shard_map.113 = (bf16[256,128]{1,0:T(8,128)(2,1)}, bf16[256,128]{1,0:T(8,128)(2,1)}) custom-call(s32[256]{0:T(256)S(1)} %copy-done.6, f32[128,256]{1,0:T(8,128)S(1)} %get-tuple-element.59.refs_0_, bf16[128,256]{1,0:T(8,128)(2,1)S(1)} %collective-permute-done.14.refs_1_, bf16[128,256]{1,0:T(8,128)(2,1)S(1)} %collective-permute-done.15.refs_2_, ...), custom_call_target="tpu_custom_call" | custom-call | bytes 2097152 | tf_op jit(solution)/shard_map/pallas_call | solution.py:27
  (13 shorter events, 0.3 us)
Async XLA Ops:
  0.6 31.8 %collective-permute-start = (bf16[256,2048]{1,0:T(8,128)(2,1)}, bf16[256,2048]{1,0:T(8,128)(2,1)S(1)}, u32[]{:S(2)}, u32[]{:S(2)}) collective-permute-start(bf16[256,2048]{1,0:T(8,128)(2,1)} %lg_ref.1), channel_id=1, source_target_pairs={{0,1},{1,0},{2,3},{3,2},{4,5},{5,4},{6,7},{7,6},{8,9},{9,8},{10,11... | collective-permute-start | bytes 3145736 | tf_op jit(solution)/shard_map/ppermute | solution.py:23
  4.2 15.6 %collective-permute-start.1 = (bf16[128,2048]{1,0:T(8,128)(2,1)}, bf16[128,2048]{1,0:T(8,128)(2,1)S(1)}, u32[]{:S(2)}, u32[]{:S(2)}) collective-permute-start(bf16[128,2048]{1,0:T(8,128)(2,1)} %get-tuple-element.38.refs_3_), channel_id=1, source_target_pairs={{0,2},{1,3},{2,0},{3,1},{4,6},{5,7},{6,4},{7,5},{8,10},{9,11},{10,... | collective-permute-start | bytes 1572872 | tf_op jit(solution)/shard_map/ppermute | solution.py:23
  6.7 24.0 %collective-permute-start.10 = (bf16[128,2048]{1,0:T(8,128)(2,1)}, bf16[128,2048]{1,0:T(8,128)(2,1)S(1)}, u32[]{:S(2)}, u32[]{:S(2)}) collective-permute-start(bf16[128,2048]{1,0:T(8,128)(2,1)} %get-tuple-element.39.refs_4_), channel_id=1, source_target_pairs={{0,2},{1,3},{2,0},{3,1},{4,6},{5,7},{6,4},{7,5},{8,10},{9,11},{10,... | collective-permute-start | bytes 1572872 | tf_op jit(solution)/shard_map/ppermute | solution.py:23
  6.8 12.9 %collective-permute-start.8 = (bf16[528,128]{1,0:T(8,128)(2,1)}, bf16[528,128]{1,0:T(8,128)(2,1)S(1)}, u32[]{:S(2)}, u32[]{:S(2)}) collective-permute-start(bf16[528,128]{1,0:T(8,128)(2,1)} %get-tuple-element.47.refs_9_), channel_id=1, source_target_pairs={{0,24},{4,28},{8,16},{12,20},{16,8},{20,12},{24,0},{28,4},{1,25},{... | collective-permute-start | bytes 405512 | tf_op jit(solution)/shard_map/ppermute | solution.py:23
  10.8 11.7 %collective-permute-start.6 = (bf16[528,128]{1,0:T(8,128)(2,1)}, bf16[528,128]{1,0:T(8,128)(2,1)S(1)}, u32[]{:S(2)}, u32[]{:S(2)}) collective-permute-start(bf16[528,128]{1,0:T(8,128)(2,1)} %get-tuple-element.47.refs_9_), channel_id=1, source_target_pairs={{0,16},{4,20},{8,24},{12,28},{16,0},{20,4},{24,8},{28,12},{1,17},{... | collective-permute-start | bytes 405512 | tf_op jit(solution)/shard_map/ppermute | solution.py:23
  19.7 32.0 %collective-permute-start.2 = (bf16[128,2048]{1,0:T(8,128)(2,1)S(1)}, bf16[128,2048]{1,0:T(8,128)(2,1)}, u32[]{:S(2)}, u32[]{:S(2)}) collective-permute-start(bf16[128,2048]{1,0:T(8,128)(2,1)S(1)} %collective-permute-done.1.refs_3_), channel_id=1, source_target_pairs={{0,1},{1,0},{2,3},{3,2},{4,5},{5,4},{6,7},{7,6},{8,9},{9,8},{10,11... | collective-permute-start | bytes 1572872 | tf_op jit(solution)/shard_map/ppermute | solution.py:23
  19.7 6.9 %collective-permute-start.4 = (bf16[528,128]{1,0:T(8,128)(2,1)}, bf16[528,128]{1,0:T(8,128)(2,1)S(1)}, u32[]{:S(2)}, u32[]{:S(2)}) collective-permute-start(bf16[528,128]{1,0:T(8,128)(2,1)} %get-tuple-element.47.refs_9_), channel_id=1, source_target_pairs={{0,8},{4,12},{8,0},{12,4},{16,24},{20,28},{24,16},{28,20},{1,9},{5... | collective-permute-start | bytes 405512 | tf_op jit(solution)/shard_map/ppermute | solution.py:23
  22.6 5.4 %collective-permute-start.3 = (bf16[528,128]{1,0:T(8,128)(2,1)}, bf16[528,128]{1,0:T(8,128)(2,1)S(1)}, u32[]{:S(2)}, u32[]{:S(2)}) collective-permute-start(bf16[528,128]{1,0:T(8,128)(2,1)} %get-tuple-element.47.refs_9_), channel_id=1, source_target_pairs={{0,4},{4,0},{8,12},{12,8},{16,20},{20,16},{24,28},{28,24},{1,5},{5... | collective-permute-start | bytes 405512 | tf_op jit(solution)/shard_map/ppermute | solution.py:23
  26.6 25.1 %collective-permute-start.9 = (bf16[528,128]{1,0:T(8,128)(2,1)S(1)}, bf16[528,128]{1,0:T(8,128)(2,1)S(1)}, u32[]{:S(2)}, u32[]{:S(2)}) collective-permute-start(bf16[528,128]{1,0:T(8,128)(2,1)S(1)} %collective-permute-done.8.refs_15_), channel_id=1, source_target_pairs={{0,4},{4,0},{8,12},{12,8},{16,20},{20,16},{24,28},{28,24},{1,5},{5... | collective-permute-start | bytes 405512 | tf_op jit(solution)/shard_map/ppermute | solution.py:23
  27.9 23.8 %collective-permute-start.7 = (bf16[528,128]{1,0:T(8,128)(2,1)S(1)}, bf16[528,128]{1,0:T(8,128)(2,1)S(1)}, u32[]{:S(2)}, u32[]{:S(2)}) collective-permute-start(bf16[528,128]{1,0:T(8,128)(2,1)S(1)} %collective-permute-done.6.refs_13_), channel_id=1, source_target_pairs={{0,4},{4,0},{8,12},{12,8},{16,20},{20,16},{24,28},{28,24},{1,5},{5... | collective-permute-start | bytes 405512 | tf_op jit(solution)/shard_map/ppermute | solution.py:23
  30.8 21.0 %collective-permute-start.5 = (bf16[528,128]{1,0:T(8,128)(2,1)S(1)}, bf16[528,128]{1,0:T(8,128)(2,1)S(1)}, u32[]{:S(2)}, u32[]{:S(2)}) collective-permute-start(bf16[528,128]{1,0:T(8,128)(2,1)S(1)} %collective-permute-done.4.refs_11_), channel_id=1, source_target_pairs={{0,4},{4,0},{8,12},{12,8},{16,20},{20,16},{24,28},{28,24},{1,5},{5... | collective-permute-start | bytes 405512 | tf_op jit(solution)/shard_map/ppermute | solution.py:23
  32.5 30.1 %collective-permute-start.11 = (bf16[128,2048]{1,0:T(8,128)(2,1)S(1)}, bf16[128,2048]{1,0:T(8,128)(2,1)S(1)}, u32[]{:S(2)}, u32[]{:S(2)}) collective-permute-start(bf16[128,2048]{1,0:T(8,128)(2,1)S(1)} %collective-permute-done.10.refs_1_), channel_id=1, source_target_pairs={{0,1},{1,0},{2,3},{3,2},{4,5},{5,4},{6,7},{7,6},{8,9},{9,8},{10,11... | collective-permute-start | bytes 1572872 | tf_op jit(solution)/shard_map/ppermute | solution.py:23
  32.5 1.0 %copy-start = (bf16[256,8,128]{2,1,0:T(8,128)(2,1)S(1)}, bf16[256,8,128]{2,1,0:T(8,128)(2,1)}, u32[]{:S(2)}) copy-start(bf16[256,8,128]{2,1,0:T(8,128)(2,1)} %param.8) | copy-start | bytes 1572868
  33.5 1.0 %copy-start.1 = (bf16[256,8,128]{2,1,0:T(8,128)(2,1)S(1)}, bf16[256,8,128]{2,1,0:T(8,128)(2,1)}, u32[]{:S(2)}) copy-start(bf16[256,8,128]{2,1,0:T(8,128)(2,1)} %param.11) | copy-start | bytes 1572868
  34.6 1.0 %copy-start.2 = (bf16[128,2048]{1,0:T(8,128)(2,1)S(1)}, bf16[128,2048]{1,0:T(8,128)(2,1)}, u32[]{:S(2)}) copy-start(bf16[128,2048]{1,0:T(8,128)(2,1)} %get-tuple-element.38.refs_3_) | copy-start | bytes 1572868
  35.6 1.0 %copy-start.3 = (bf16[128,2048]{1,0:T(8,128)(2,1)S(1)}, bf16[128,2048]{1,0:T(8,128)(2,1)}, u32[]{:S(2)}) copy-start(bf16[128,2048]{1,0:T(8,128)(2,1)} %get-tuple-element.39.refs_4_) | copy-start | bytes 1572868
  36.7 0.7 copy-start.5
  37.3 0.7 copy-start.7
  49.9 1.8 %copy-start.4 = (bf16[528,128]{1,0:T(8,128)(2,1)S(1)}, bf16[528,128]{1,0:T(8,128)(2,1)}, u32[]{:S(2)}) copy-start(bf16[528,128]{1,0:T(8,128)(2,1)} %get-tuple-element.47.refs_9_) | copy-start | bytes 405508
  49.9 1.8 %copy-start.6 = (s32[256]{0:T(256)S(1)}, s32[256]{0:T(256)}, u32[]{:S(2)}) copy-start(s32[256]{0:T(256)} %pos_ref.3) | copy-start | bytes 3076
  66.9 6.4 %collective-permute-start.12 = (bf16[256,256]{1,0:T(8,128)(2,1)S(1)}, bf16[256,256]{1,0:T(8,128)(2,1)S(1)}, u32[]{:S(2)}, u32[]{:S(2)}) collective-permute-start(bf16[256,256]{1,0:T(8,128)(2,1)S(1)} %get-tuple-element.58), channel_id=1, source_target_pairs={{0,4},{4,0},{8,12},{12,8},{16,20},{20,16},{24,28},{28,24},{1,5},{5... | collective-permute-start | bytes 393224 | tf_op jit(solution)/shard_map/ppermute | solution.py:23
  67.3 8.9 %collective-permute-start.13 = (bf16[256,256]{1,0:T(8,128)(2,1)S(1)}, bf16[256,256]{1,0:T(8,128)(2,1)S(1)}, u32[]{:S(2)}, u32[]{:S(2)}) collective-permute-start(bf16[256,256]{1,0:T(8,128)(2,1)S(1)} %get-tuple-element.60), channel_id=1, source_target_pairs={{0,4},{4,0},{8,12},{12,8},{16,20},{20,16},{24,28},{28,24},{1,5},{5... | collective-permute-start | bytes 393224 | tf_op jit(solution)/shard_map/ppermute | solution.py:23
  69.0 11.2 %collective-permute-start.17 = (bf16[256,256]{1,0:T(8,128)(2,1)S(1)}, bf16[256,256]{1,0:T(8,128)(2,1)S(1)}, u32[]{:S(2)}, u32[]{:S(2)}) collective-permute-start(bf16[256,256]{1,0:T(8,128)(2,1)S(1)} %get-tuple-element.65), channel_id=1, source_target_pairs={{0,4},{4,0},{8,12},{12,8},{16,20},{20,16},{24,28},{28,24},{1,5},{5... | collective-permute-start | bytes 393224 | tf_op jit(solution)/shard_map/ppermute | solution.py:23
  69.3 11.9 %collective-permute-start.18 = (bf16[256,256]{1,0:T(8,128)(2,1)S(1)}, bf16[256,256]{1,0:T(8,128)(2,1)S(1)}, u32[]{:S(2)}, u32[]{:S(2)}) collective-permute-start(bf16[256,256]{1,0:T(8,128)(2,1)S(1)} %get-tuple-element.67), channel_id=1, source_target_pairs={{0,4},{4,0},{8,12},{12,8},{16,20},{20,16},{24,28},{28,24},{1,5},{5... | collective-permute-start | bytes 393224 | tf_op jit(solution)/shard_map/ppermute | solution.py:23
  73.4 10.6 %collective-permute-start.16 = (bf16[128,256]{1,0:T(8,128)(2,1)S(1)}, bf16[128,256]{1,0:T(8,128)(2,1)S(1)}, u32[]{:S(2)}, u32[]{:S(2)}) collective-permute-start(bf16[128,256]{1,0:T(8,128)(2,1)S(1)} %get-tuple-element.63), channel_id=1, source_target_pairs={{0,8},{4,12},{8,0},{12,4},{16,24},{20,28},{24,16},{28,20},{1,9},{5... | collective-permute-start | bytes 196616 | tf_op jit(solution)/shard_map/ppermute | solution.py:23
  76.2 10.3 %collective-permute-start.14 = (bf16[128,256]{1,0:T(8,128)(2,1)S(1)}, bf16[128,256]{1,0:T(8,128)(2,1)S(1)}, u32[]{:S(2)}, u32[]{:S(2)}) collective-permute-start(bf16[128,256]{1,0:T(8,128)(2,1)S(1)} %get-tuple-element.61), channel_id=1, source_target_pairs={{0,16},{4,20},{8,24},{12,28},{16,0},{20,4},{24,8},{28,12},{1,17},{... | collective-permute-start | bytes 196616 | tf_op jit(solution)/shard_map/ppermute | solution.py:23
  78.8 7.7 %collective-permute-start.15 = (bf16[128,256]{1,0:T(8,128)(2,1)S(1)}, bf16[128,256]{1,0:T(8,128)(2,1)S(1)}, u32[]{:S(2)}, u32[]{:S(2)}) collective-permute-start(bf16[128,256]{1,0:T(8,128)(2,1)S(1)} %get-tuple-element.62), channel_id=1, source_target_pairs={{0,24},{4,28},{8,16},{12,20},{16,8},{20,12},{24,0},{28,4},{1,25},{... | collective-permute-start | bytes 196616 | tf_op jit(solution)/shard_map/ppermute | solution.py:23
  80.2 6.3 %collective-permute-start.21 = (bf16[128,256]{1,0:T(8,128)(2,1)S(1)}, bf16[128,256]{1,0:T(8,128)(2,1)S(1)}, u32[]{:S(2)}, u32[]{:S(2)}) collective-permute-start(bf16[128,256]{1,0:T(8,128)(2,1)S(1)} %get-tuple-element.70), channel_id=1, source_target_pairs={{0,8},{4,12},{8,0},{12,4},{16,24},{20,28},{24,16},{28,20},{1,9},{5... | collective-permute-start | bytes 196616 | tf_op jit(solution)/shard_map/ppermute | solution.py:23
  81.3 7.2 %collective-permute-start.19 = (bf16[128,256]{1,0:T(8,128)(2,1)S(1)}, bf16[128,256]{1,0:T(8,128)(2,1)S(1)}, u32[]{:S(2)}, u32[]{:S(2)}) collective-permute-start(bf16[128,256]{1,0:T(8,128)(2,1)S(1)} %get-tuple-element.68), channel_id=1, source_target_pairs={{0,16},{4,20},{8,24},{12,28},{16,0},{20,4},{24,8},{28,12},{1,17},{... | collective-permute-start | bytes 196616 | tf_op jit(solution)/shard_map/ppermute | solution.py:23
  84.0 6.2 %collective-permute-start.20 = (bf16[128,256]{1,0:T(8,128)(2,1)S(1)}, bf16[128,256]{1,0:T(8,128)(2,1)S(1)}, u32[]{:S(2)}, u32[]{:S(2)}) collective-permute-start(bf16[128,256]{1,0:T(8,128)(2,1)S(1)} %get-tuple-element.69), channel_id=1, source_target_pairs={{0,24},{4,28},{8,16},{12,20},{16,8},{20,12},{24,0},{28,4},{1,25},{... | collective-permute-start | bytes 196616 | tf_op jit(solution)/shard_map/ppermute | solution.py:23
